TPU v7x, 32 devices: a whole 2x2x4 slice. The times are simulated.
32 devices in a mesh: seq: 2 (over core), hid: 4 (over y, x), wid: 4 (over z).
Axes of the slice: x: 2, y: 2, z: 4, core: 2. Of those that a mesh axis runs over, the one named last changes fastest.
Arguments:
- inputs: bfloat16 [2048, 1536], P(('seq', 'hid'), 'wid'), may hold values from -6 to 6
- gain_attn: bfloat16 [1536], P('wid'), may hold values from 0.5 to 1.5
- gain_ffn: bfloat16 [1536], P('wid'), may hold values from 0.5 to 1.5
- w_query: bfloat16 [1536, 1536], P(None, 'wid'), may hold values from -0.15625 to 0.15625
- w_key: bfloat16 [1536, 1536], P(None, 'wid'), may hold values from -0.15625 to 0.15625
- w_value: bfloat16 [1536, 1536], P(None, 'wid'), may hold values from -0.15625 to 0.15625
- w_house: bfloat16 [1536, 1536], P(None, 'wid'), may hold values from -0.15625 to 0.15625
- w_beta: bfloat16 [1536, 12], P(None, 'wid'), may hold values from -0.15625 to 0.15625
- w_out: bfloat16 [1536, 1536], P('wid'), may hold values from -0.625 to 0.625
- w_gate: bfloat16 [1536, 4096], P(None, ('hid', 'wid')), may hold values from -0.15625 to 0.15625
- w_up: bfloat16 [1536, 4096], P(None, ('hid', 'wid')), may hold values from -0.15625 to 0.15625
- w_down: bfloat16 [4096, 1536], P(('hid', 'wid')), may hold values from -0.09375 to 0.09375
- lengths: int32 [3], replicated, may hold values from 1 to 1024, 2048 in all
- cotangent: bfloat16 [2048, 1536], P(('seq', 'hid'), 'wid'), may hold values from -6 to 6
Outputs:
- output: bfloat16 [2048, 1536], P(('seq', 'hid'), 'wid')
- d_inputs: float32 [2048, 1536], P(('seq', 'hid'), 'wid')
- d_gain_attn: float32 [1536], P(('seq', 'hid'))
- d_gain_ffn: float32 [1536], P(('seq', 'hid'))
- d_query: float32 [1536, 1536], P(('seq', 'hid'), 'wid')
- d_key: float32 [1536, 1536], P(('seq', 'hid'), 'wid')
- d_value: float32 [1536, 1536], P(('seq', 'hid'), 'wid')
- d_house: float32 [1536, 1536], P(('seq', 'hid'), 'wid')
- d_beta: float32 [1536, 12], P(('seq', 'hid'), 'wid')
- d_out: float32 [1536, 1536], P('wid', ('seq', 'hid'))
- d_gate: float32 [1536, 4096], P('seq', ('hid', 'wid'))
- d_up: float32 [1536, 4096], P('seq', ('hid', 'wid'))
- d_down: float32 [4096, 1536], P(('hid', 'wid'), 'seq')
Inputs may be any that keep to these rules, and one draw needn't show every extreme that they name: `lengths`: the 3 documents are packed in order and fill all 2048 tokens; the longest has exactly 1024 tokens.
All inputs are finite; a program needn't handle non-finite values.
Results may differ from a plain program's by a relative error of at most 0.014.
Values may be sent and summed in bfloat16 or wider, within the bound.
A program may use at most 448 MiB of HBM per device.

v0:
```python
import jax
import jax.numpy as jnp
from jax import lax
from jax.sharding import PartitionSpec as P

HDIM = 128
LEAST = 1024


eps_norm = 1e-06
neg_big = -1e30
highest = lax.Precision.HIGHEST


def shifted(array, axis, by):
    peers = lax.axis_size(axis)
    pairs = [(i, i + by) for i in range(peers) if 0 <= i + by < peers]
    return lax.ppermute(array, axis, pairs)


def unit_lower_inverse(matrix):
    heads_n = matrix.shape[0]
    size_n = matrix.shape[1]
    full_n = 1
    while full_n < size_n:
        full_n = full_n * 2
    inverse = jnp.ones((heads_n, full_n, 1, 1), jnp.float32)
    span = 1
    while span < full_n:
        count = full_n // (2 * span)
        shaped = matrix.reshape(heads_n, count, 2 * span, count, 2 * span)
        picker = jnp.eye(count, dtype=jnp.float32)
        diag_blocks = jnp.einsum("hiajb,ij->hiab", shaped, picker, precision=highest)
        corner = diag_blocks[:, :, span:, :span]
        pairs = inverse.reshape(heads_n, count, 2, span, span)
        first = pairs[:, :, 0]
        second = pairs[:, :, 1]
        partial_left = jnp.einsum("hiab,hibc->hiac", corner, first, precision=highest)
        lower_left = -jnp.einsum("hiab,hibc->hiac", second, partial_left, precision=highest)
        blanks = jnp.zeros((heads_n, count, span, span), jnp.float32)
        upper_half = jnp.concatenate([first, blanks], 3)
        lower_half = jnp.concatenate([lower_left, second], 3)
        inverse = jnp.concatenate([upper_half, lower_half], 2)
        span = span * 2
    return inverse.reshape(heads_n, full_n, full_n)


def doc_index(positions, lengths):
    ends_at = jnp.cumsum(lengths)
    return jnp.sum((positions[:, None] >= ends_at[None, :]).astype(jnp.int32), 1)


def heads_split(matrix, head_count):
    rows_n = matrix.shape[0]
    return matrix.reshape(rows_n, head_count, -1).transpose(1, 0, 2)


def heads_merge(tensor):
    return tensor.transpose(1, 0, 2).reshape(tensor.shape[1], -1)


def norm_rows(hidden_f):
    inverse = lax.rsqrt(jnp.mean(hidden_f * hidden_f, -1, keepdims=True) + eps_norm)
    return (hidden_f * inverse, inverse)


def norm_back(grad_out, normed, inverse, gain_vec):
    scaled_grad = grad_out * gain_vec
    grad_gain = jnp.sum(grad_out * normed, 0)
    grad_in = inverse * (scaled_grad - normed * jnp.mean(scaled_grad * normed, -1, keepdims=True))
    return (grad_in, grad_gain)


def path_block(queries, key_rows, house_raw, beta_raw):
    length = queries.shape[1]
    head_dim = queries.shape[2]
    beta_vals = 2.0 * jax.nn.sigmoid(beta_raw)
    unit_dirs = house_raw * lax.rsqrt(jnp.sum(house_raw * house_raw, -1, keepdims=True) + eps_norm)
    gram_mat = jnp.einsum("htd,hsd->hts", unit_dirs, unit_dirs, precision=highest)
    identity = jnp.eye(length, dtype=jnp.float32)
    lower_sys = identity + jnp.tril(gram_mat, -1) * beta_vals[:, None, :]
    upper_sys = identity + jnp.triu(gram_mat, 1) * beta_vals[:, None, :]
    lower_inv = unit_lower_inverse(lower_sys)
    upper_inv_t = unit_lower_inverse(upper_sys.transpose(0, 2, 1))
    unit_keys = jnp.einsum("htd,hjd->htj", unit_dirs, key_rows, precision=highest)
    unit_query = jnp.einsum("htd,hid->hti", unit_dirs, queries, precision=highest)
    carried = jnp.einsum("hts,hsj->htj", lower_inv, jnp.tril(unit_keys, -1), precision=highest)
    forward_part = jnp.einsum("hst,hsi->hti", upper_inv_t, jnp.triu(unit_query), precision=highest)
    scaled = beta_vals[:, :, None] * unit_dirs
    keys_out = key_rows - jnp.einsum("htj,htd->hjd", carried, scaled, precision=highest)
    query_out = queries - jnp.einsum("hti,htd->hid", forward_part, scaled, precision=highest)
    direct = jnp.einsum("hid,hjd->hij", queries, key_rows, precision=highest)
    through = jnp.einsum(
        "hti,htj->hij", jnp.triu(unit_query), beta_vals[:, :, None] * carried, precision=highest
    )
    near_raw = direct - through
    solved = jnp.einsum("hts,hsd->htd", lower_inv, unit_dirs, precision=highest)
    product = jnp.eye(head_dim, dtype=jnp.float32) - jnp.einsum(
        "htd,hte->hde", scaled, solved, precision=highest
    )
    return (query_out, keys_out, near_raw, product)


def body(
    inputs,
    gain_attn,
    gain_ffn,
    w_query,
    w_key,
    w_value,
    w_house,
    w_beta,
    w_out,
    w_gate,
    w_up,
    w_down,
    lengths,
    cotangent,
):
    tok_dev = inputs.shape[0]
    col_dev = inputs.shape[1]
    wid_n = lax.axis_size("wid")
    hid_n = lax.axis_size("hid")
    row_devs = lax.axis_size(("seq", "hid"))
    my_row = lax.axis_index(("seq", "hid"))
    my_hid = lax.axis_index("hid")
    my_wid = lax.axis_index("wid")
    tokens_all = tok_dev * row_devs
    most_len = max(LEAST, 2 * tokens_all // 5)
    hop_count = min((most_len - 2) // tok_dev + 1, row_devs - 1)
    head_dim = HDIM
    heads_dev = w_query.shape[1] // head_dim
    ff_dev = w_gate.shape[1]
    score_scale = head_dim ** (-0.5)
    whole_x, gain_one, gain_two = (
        lax.all_gather(inputs, "wid", axis=1, tiled=True),
        lax.all_gather(gain_attn, "wid", axis=0, tiled=True),
        lax.all_gather(gain_ffn, "wid", axis=0, tiled=True),
    )
    model_dim = whole_x.shape[1]
    residual = whole_x.astype(jnp.float32)
    gain_one = gain_one.astype(jnp.float32)
    gain_two = gain_two.astype(jnp.float32)
    normed_one, inverse_one = norm_rows(residual)
    act_in = (normed_one * gain_one).astype(jnp.bfloat16)

    def project(weight):
        return jnp.dot(act_in, weight, preferred_element_type=jnp.float32)

    q_heads = heads_split(project(w_query), heads_dev)
    k_heads = heads_split(project(w_key), heads_dev)
    values_low = heads_split(project(w_value), heads_dev).astype(jnp.bfloat16)
    house_heads = heads_split(project(w_house), heads_dev)
    beta_heads = project(w_beta).T
    (query_out, keys_out, near_raw, product), path_back = jax.vjp(
        path_block, q_heads, k_heads, house_heads, beta_heads
    )
    offsets = jnp.arange(tok_dev, dtype=jnp.int32)
    own_docs = doc_index(my_row * tok_dev + offsets, lengths)
    causal = offsets[:, None] >= offsets[None, :]
    near_mask = causal & (own_docs[:, None] == own_docs[None, :])
    near_scores = jnp.where(near_mask[None], near_raw * score_scale, neg_big)
    query_low = query_out.astype(jnp.bfloat16)

    def far_scores(key_block, distance):
        source = my_row - distance
        docs_far = doc_index(source * tok_dev + offsets, lengths)
        docs_far = jnp.where(source >= 0, docs_far, -1)
        allowed = own_docs[:, None] == docs_far[None, :]
        raw_scores = jnp.einsum(
            "hid,hjd->hij", query_low, key_block, preferred_element_type=jnp.float32
        )
        return jnp.where(allowed[None], raw_scores * score_scale, neg_big)

    def hop_step(hop_state, distance):
        sent_keys, sent_vals = hop_state
        got_keys, got_vals = shifted((sent_keys, sent_vals), ("seq", "hid"), 1)
        moved = jnp.einsum(
            "hjd,hed->hje", got_keys.astype(jnp.float32), product, precision=highest
        ).astype(jnp.bfloat16)
        return ((moved, got_vals), (got_keys, got_vals))

    distances = jnp.arange(1, hop_count + 1, dtype=jnp.int32)
    last_sent, (far_keys, far_vals) = lax.scan(
        hop_step, (keys_out.astype(jnp.bfloat16), values_low), distances
    )
    run_max = jnp.max(near_scores, -1)
    run_sum = jnp.sum(jnp.exp(near_scores - run_max[..., None]), -1)

    def stat_step(stat_state, inputs_hop):
        key_block, distance = inputs_hop
        prev_max, prev_sum = stat_state
        scores = far_scores(key_block, distance)
        new_max = jnp.maximum(prev_max, jnp.max(scores, -1))
        new_sum = prev_sum * jnp.exp(prev_max - new_max) + jnp.sum(
            jnp.exp(scores - new_max[..., None]), -1
        )
        return ((new_max, new_sum), scores)

    (run_max, run_sum), kept_scores = lax.scan(stat_step, (run_max, run_sum), (far_keys, distances))
    log_total = run_max + jnp.log(run_sum)
    near_probs = jnp.exp(near_scores - log_total[..., None])
    attended = jnp.einsum(
        "hij,hjd->hid",
        near_probs.astype(jnp.bfloat16),
        values_low,
        preferred_element_type=jnp.float32,
    )

    def out_step(running, inputs_hop):
        score_block, val_block = inputs_hop
        prob_vals = jnp.exp(score_block - log_total[..., None]).astype(jnp.bfloat16)
        return (
            running
            + jnp.einsum("hij,hjd->hid", prob_vals, val_block, preferred_element_type=jnp.float32),
            None,
        )

    attended, unused_out = lax.scan(out_step, attended, (kept_scores, far_vals))
    attn_low = heads_merge(attended).astype(jnp.bfloat16)
    attn_part = jnp.dot(attn_low, w_out, preferred_element_type=jnp.float32)
    mixed = residual + lax.psum(attn_part, "wid")
    normed_two, inverse_two = norm_rows(mixed)
    inner_low = (normed_two * gain_two).astype(jnp.bfloat16)
    inner_all = lax.all_gather(inner_low, "hid", axis=0, tiled=True)
    gate_up = jnp.concatenate([w_gate, w_up], 1)
    pre_act = jnp.dot(inner_all, gate_up, preferred_element_type=jnp.float32)
    gate_val = pre_act[:, :ff_dev]
    up_val = pre_act[:, ff_dev:]
    hidden = (jax.nn.silu(gate_val) * up_val).astype(jnp.bfloat16)
    mixed_cols = lax.dynamic_slice_in_dim(mixed, my_wid * col_dev, col_dev, 1)

    def one_slot(offset):
        rows_of = lax.dynamic_slice_in_dim(hidden, offset // wid_n * tok_dev, tok_dev, 0)
        cols_of = lax.dynamic_slice_in_dim(w_down, offset % wid_n * col_dev, col_dev, 1)
        return jnp.dot(rows_of, cols_of, preferred_element_type=jnp.float32)

    blocks = lax.map(
        one_slot, jnp.arange(tok_dev * lax.axis_size(("hid", "wid")) // tok_dev, dtype=jnp.int32)
    )
    ffn_out = lax.psum_scatter(
        blocks.reshape(tok_dev * lax.axis_size(("hid", "wid")), col_dev).astype(jnp.bfloat16),
        ("hid", "wid"),
        scatter_dimension=0,
        tiled=True,
    ).astype(jnp.float32)
    output = (mixed_cols + ffn_out).astype(jnp.bfloat16)
    rows_all = hid_n * tok_dev
    dy_blocks = cotangent[None]
    start_state = (
        jnp.zeros((rows_all, ff_dev), jnp.float32),
        jnp.zeros((ff_dev, model_dim), jnp.float32),
        jnp.zeros((tok_dev, model_dim), jnp.float32),
    )
    shard_rows = lax.all_gather(dy_blocks, ("hid", "wid"), axis=0, tiled=True)

    def one_piece(offset, piece_state):
        grad_hidden, grad_down, own_dy = piece_state
        row_blk = offset // wid_n
        col_blk = offset % wid_n
        dy_block = lax.dynamic_index_in_dim(shard_rows, offset, 0, keepdims=False)
        cols_of = lax.dynamic_slice_in_dim(w_down, col_blk * col_dev, col_dev, 1)
        rows_of = lax.dynamic_slice_in_dim(hidden, row_blk * tok_dev, tok_dev, 0)
        add_hidden = jnp.einsum("tc,fc->tf", dy_block, cols_of, preferred_element_type=jnp.float32)
        current = lax.dynamic_slice_in_dim(grad_hidden, row_blk * tok_dev, tok_dev, 0)
        grad_hidden = lax.dynamic_update_slice_in_dim(
            grad_hidden, current + add_hidden, row_blk * tok_dev, 0
        )
        add_down = jnp.einsum("tf,tc->fc", rows_of, dy_block, preferred_element_type=jnp.float32)
        current_d = lax.dynamic_slice_in_dim(grad_down, col_blk * col_dev, col_dev, 1)
        grad_down = lax.dynamic_update_slice_in_dim(
            grad_down, current_d + add_down, col_blk * col_dev, 1
        )
        current_y = lax.dynamic_slice_in_dim(own_dy, col_blk * col_dev, col_dev, 1)
        fresh_y = jnp.where(row_blk == my_hid, dy_block.astype(jnp.float32), current_y)
        own_dy = lax.dynamic_update_slice_in_dim(own_dy, fresh_y, col_blk * col_dev, 1)
        return (grad_hidden, grad_down, own_dy)

    grad_hidden, grad_down, own_dy = lax.fori_loop(0, shard_rows.shape[0], one_piece, start_state)
    sig_gate = jax.nn.sigmoid(gate_val)
    grad_gate = grad_hidden * up_val * sig_gate * (1.0 + gate_val * (1.0 - sig_gate))
    grad_up = grad_hidden * gate_val * sig_gate
    grad_pre = jnp.concatenate([grad_gate, grad_up], 1).astype(jnp.bfloat16)
    grad_gate_up = jnp.einsum("tc,tf->cf", inner_all, grad_pre, preferred_element_type=jnp.float32)
    rows_of = grad_pre
    inner_rows = lax.psum_scatter(
        jnp.einsum("tf,cf->tc", rows_of, gate_up, preferred_element_type=jnp.float32),
        "hid",
        scatter_dimension=0,
        tiled=True,
    )
    grad_inner = lax.psum(inner_rows, "wid")
    grad_mixed_n, grad_gain_two = norm_back(grad_inner, normed_two, inverse_two, gain_two)
    grad_mixed = own_dy + grad_mixed_n
    grad_z = grad_mixed.astype(jnp.bfloat16)
    grad_w_out = jnp.einsum("ti,tc->ic", attn_low, grad_z, preferred_element_type=jnp.float32)
    grad_attn = heads_split(
        jnp.einsum("tc,ic->ti", grad_z, w_out, preferred_element_type=jnp.float32), heads_dev
    ).astype(jnp.bfloat16)
    near_dp = jnp.einsum("hid,hjd->hij", grad_attn, values_low, preferred_element_type=jnp.float32)
    row_delta = jnp.sum(near_probs * near_dp, -1)

    def delta_step(running, inputs_hop):
        score_block, val_block = inputs_hop
        prob_vals = jnp.exp(score_block - log_total[..., None])
        dprob_vals = jnp.einsum(
            "hid,hjd->hij", grad_attn, val_block, preferred_element_type=jnp.float32
        )
        return (running + jnp.sum(prob_vals * dprob_vals, -1), dprob_vals)

    row_delta, kept_dprob = lax.scan(delta_step, row_delta, (kept_scores, far_vals))
    near_ds = near_probs * (near_dp - row_delta[..., None]) * score_scale
    grad_vals = jnp.einsum(
        "hij,hid->hjd",
        near_probs.astype(jnp.bfloat16),
        grad_attn,
        preferred_element_type=jnp.float32,
    )

    def back_step(back_state, inputs_hop):
        recv_keys, recv_vals, grad_query, grad_prod = back_state
        key_block, score_block, dprob_vals = inputs_hop
        prob_vals = jnp.exp(score_block - log_total[..., None])
        dscore = (prob_vals * (dprob_vals - row_delta[..., None]) * score_scale).astype(
            jnp.bfloat16
        )
        grad_query = grad_query + jnp.einsum(
            "hij,hjd->hid", dscore, key_block, preferred_element_type=jnp.float32
        )
        key_grad = jnp.einsum("hij,hid->hjd", dscore, query_low, preferred_element_type=jnp.float32)
        key_grad = key_grad + jnp.einsum("hje,hed->hjd", recv_keys, product, precision=highest)
        grad_prod = grad_prod + jnp.einsum(
            "hje,hjd->hed", recv_keys, key_block.astype(jnp.float32), precision=highest
        )
        val_grad = (
            jnp.einsum(
                "hij,hid->hjd",
                prob_vals.astype(jnp.bfloat16),
                grad_attn,
                preferred_element_type=jnp.float32,
            )
            + recv_vals
        )
        sent_keys, sent_vals = shifted((key_grad, val_grad), ("seq", "hid"), -1)
        return ((sent_keys, sent_vals, grad_query, grad_prod), None)

    zero_heads = jnp.zeros((heads_dev, tok_dev, head_dim), jnp.float32)
    back_start = (
        zero_heads,
        zero_heads,
        zero_heads,
        jnp.zeros((heads_dev, head_dim, head_dim), jnp.float32),
    )
    (tail_keys, tail_vals, grad_query, grad_prod), unused_back = lax.scan(
        back_step, back_start, (far_keys, kept_scores, kept_dprob), reverse=True
    )
    grad_q, grad_k, grad_house, grad_beta = path_back((grad_query, tail_keys, near_ds, grad_prod))
    grad_q_low = heads_merge(grad_q).astype(jnp.bfloat16)
    grad_k_low = heads_merge(grad_k).astype(jnp.bfloat16)
    grad_v_low = heads_merge(grad_vals + tail_vals).astype(jnp.bfloat16)
    grad_h_low = heads_merge(grad_house).astype(jnp.bfloat16)
    grad_b_low = grad_beta.T.astype(jnp.bfloat16)

    def weight_grad(grad_low):
        return jnp.einsum("tc,ti->ci", act_in, grad_low, preferred_element_type=jnp.float32)

    def input_grad(grad_low, weight):
        return jnp.einsum("ti,ci->tc", grad_low, weight, preferred_element_type=jnp.float32)

    grad_act = (
        input_grad(grad_q_low, w_query)
        + input_grad(grad_k_low, w_key)
        + input_grad(grad_v_low, w_value)
    )
    grad_act = grad_act + input_grad(grad_h_low, w_house) + input_grad(grad_b_low, w_beta)
    grad_act = lax.psum(grad_act, "wid")
    grad_resid_n, grad_gain_one = norm_back(grad_act, normed_one, inverse_one, gain_one)
    grad_full = grad_mixed + grad_resid_n
    d_inputs = lax.dynamic_slice_in_dim(grad_full, my_wid * col_dev, col_dev, 1)
    attn_sums = (
        lax.psum_scatter(grad_gain_one, ("seq", "hid"), scatter_dimension=0, tiled=True),
        lax.psum_scatter(grad_gain_two, ("seq", "hid"), scatter_dimension=0, tiled=True),
        lax.psum_scatter(weight_grad(grad_q_low), ("seq", "hid"), scatter_dimension=0, tiled=True),
        lax.psum_scatter(weight_grad(grad_k_low), ("seq", "hid"), scatter_dimension=0, tiled=True),
        lax.psum_scatter(weight_grad(grad_v_low), ("seq", "hid"), scatter_dimension=0, tiled=True),
        lax.psum_scatter(weight_grad(grad_h_low), ("seq", "hid"), scatter_dimension=0, tiled=True),
        lax.psum_scatter(weight_grad(grad_b_low), ("seq", "hid"), scatter_dimension=0, tiled=True),
        lax.psum_scatter(grad_w_out, ("seq", "hid"), scatter_dimension=1, tiled=True),
    )
    ffn_sums = (
        lax.psum_scatter(grad_gate_up[:, :ff_dev], "seq", scatter_dimension=0, tiled=True),
        lax.psum_scatter(grad_gate_up[:, ff_dev:], "seq", scatter_dimension=0, tiled=True),
        lax.psum_scatter(grad_down, "seq", scatter_dimension=1, tiled=True),
    )
    return (
        output,
        d_inputs,
        attn_sums[0],
        attn_sums[1],
        attn_sums[2],
        attn_sums[3],
        attn_sums[4],
        attn_sums[5],
        attn_sums[6],
        attn_sums[7],
        ffn_sums[0],
        ffn_sums[1],
        ffn_sums[2],
    )


def solution(mesh):
    in_specs = (
        P(("seq", "hid"), "wid"),
        P("wid"),
        P("wid"),
        P(None, "wid"),
        P(None, "wid"),
        P(None, "wid"),
        P(None, "wid"),
        P(None, "wid"),
        P("wid", None),
        P(None, ("hid", "wid")),
        P(None, ("hid", "wid")),
        P(("hid", "wid"), None),
        P(),
        P(("seq", "hid"), "wid"),
    )
    out_specs = (
        P(("seq", "hid"), "wid"),
        P(("seq", "hid"), "wid"),
        P(("seq", "hid")),
        P(("seq", "hid")),
        P(("seq", "hid"), "wid"),
        P(("seq", "hid"), "wid"),
        P(("seq", "hid"), "wid"),
        P(("seq", "hid"), "wid"),
        P(("seq", "hid"), "wid"),
        P("wid", ("seq", "hid")),
        P("seq", ("hid", "wid")),
        P("seq", ("hid", "wid")),
        P(("hid", "wid"), "seq"),
    )
    return jax.shard_map(body, mesh=mesh, in_specs=in_specs, out_specs=out_specs, check_vma=False)
```

profile of v0, /device:TPU:0, one launch (start us, length us, event | category | flops | bytes accessed | tf_op | source)
XLA Modules:
  0.0 1950.2 jit_solution(806330628941881261)
XLA Ops:
  94.8 28.1 %reshape.555 = f32[3,64,4,64,4]{4,3,2,1,0:T(8,128)} reshape(f32[3,256,256]{2,1,0:T(8,128)} %get-tuple-element.1280) | data formatting | bytes 1572864 | tf_op jit(solution)/shard_map/jvp()/reshape | solution.py:31
  122.9 27.3 %reshape.537 = f32[3,64,4,64,4]{4,3,2,1,0:T(8,128)} reshape(f32[3,256,256]{2,1,0:T(8,128)S(1)} %get-tuple-element.1281) | data formatting | bytes 1572864 | tf_op jit(solution)/shard_map/jvp()/reshape | solution.py:31
  150.2 52.4 %reshape.553 = f32[3,128,2,128,2]{4,3,2,1,0:T(8,128)} reshape(f32[3,256,256]{2,1,0:T(8,128)} %get-tuple-element.1280) | data formatting | bytes 1572864 | tf_op jit(solution)/shard_map/jvp()/reshape | solution.py:31
  202.6 51.8 %reshape.535 = f32[3,128,2,128,2]{4,3,2,1,0:T(8,128)} reshape(f32[3,256,256]{2,1,0:T(8,128)S(1)} %get-tuple-element.1281) | data formatting | bytes 1572864 | tf_op jit(solution)/shard_map/jvp()/reshape | solution.py:31
  465.1 65.0 %while.107 = (s32[]{:T(128)}, bf16[3,256,128]{2,1,0:T(8,128)(2,1)}, bf16[3,256,128]{2,1,0:T(8,128)(2,1)}, bf16[4,3,256,128]{3,2,1,0:T(8,128)(2,1)}, bf16[4,3,256...) while((s32[]{:T(128)}, bf16[3,256,128]{2,1,0:T(8,128)(2,1)}, ...), condition=%wide.region_7.8_spmd, body=%wide.region_6.7_spmd.sunk | while | flops 151093248 | bytes 3342509 | solution.py:184
  532.0 23.2 %while.112 = (s32[]{:T(128)}, f32[3,256]{1,0:T(4,128)S(1)}, f32[3,256]{1,0:T(4,128)}, f32[4,3,256,256]{2,3,1,0:T(8,128)}, s32[256]{0:T(256)}, /*index=5*/s32[4]{...) while((s32[]{:T(128)}, f32[3,256]{1,0:T(4,128)S(1)}, ...), condition=%wide.region_12.13_spmd.clone, body=%wide.region_8.12_spmd.clone.sunk | while | flops 51384324 | bytes 3741955 | solution.py:200
  586.5 57.1 %all-reduce.67.cloned.1.call-done = f32[256,1536]{1,0:T(8,128)} async-done(((f32[256,1536]{1,0:T(8,128)}), f32[256,1536]{1,0:T(8,128)}) %all-reduce.67.cloned.1.call-update) | async-done | bytes 1572880 | tf_op jit(solution)/shard_map/psum | solution.py:222
  651.2 39.6 %all-gather.6.cloned.1.call-done = bf16[1024,1536]{1,0:T(8,128)(2,1)} async-done(((bf16[256,1536]{1,0:T(8,128)(2,1)}), bf16[1024,1536]{1,0:T(8,128)(2,1)}) %all-gather.6.cloned.1.call-update) | async-done | bytes 3145744 | tf_op jit(solution)/shard_map/all_gather | solution.py:225
  697.7 64.0 %all-gather.8.cloned.1.call-done = bf16[4096,384]{1,0:T(8,128)(2,1)} async-done(((bf16[256,384]{1,0:T(8,128)(2,1)}), bf16[4096,384]{1,0:T(8,128)(2,1)}) %all-gather.8.cloned.1.call-update) | async-done | bytes 3145744 | tf_op jit(solution)/shard_map/all_gather | solution.py:255
  765.5 117.9 %while.110 = (s32[]{:T(128)}, f32[1024,256]{0,1:T(8,128)}, f32[256,1536]{1,0:T(8,128)}, f32[256,1536]{1,0:T(8,128)}, bf16[16,256,384]{2,1,0:T(8,128)(2,1)}, /*in...) while((s32[]{:T(128)}, f32[1024,256]{0,1:T(8,128)}, ...), condition=%wide.region_21.22_spmd, body=%wide.region_20.21_spmd.sunk | while | flops 101023760 | bytes 5112234 | solution.py:279
  896.7 64.4 %reduce-scatter.16.cloned.1.call-done = f32[256,1536]{1,0:T(8,128)} async-done(((f32[1024,1536]{1,0:T(8,128)}), f32[256,1536]{1,0:T(8,128)}) %reduce-scatter.16.cloned.1.call-update) | async-done | bytes 1572880 | tf_op jit(solution)/shard_map/reduce_scatter | solution.py:286
  961.2 81.8 %while.109 = (s32[]{:T(128)}, bf16[16,256,384]{2,1,0:T(8,128)(2,1)}, s32[16]{0:T(128)S(1)}, bf16[1024,256]{1,0:T(8,128)(2,1)}, bf16[256,1536]{1,0:T(8,128)(2,1)}...) while((s32[]{:T(128)}, bf16[16,256,384]{2,1,0:T(8,128)(2,1)}, ...), condition=%wide.region_18.19_spmd, body=%wide.region_17.18_spmd.sunk | while | flops 50331676 | bytes 721348 | solution.py:238
  1066.8 102.2 %while.113 = (s32[]{:T(128)}, f32[3,256,128]{2,1,0:T(8,128)S(1)}, f32[3,256,128]{2,1,0:T(8,128)}, f32[3,256,128]{2,1,0:T(8,128)}, f32[3,128,128]{1,2,0:T(8,128)}...) while((s32[]{:T(128)}, f32[3,256,128]{2,1,0:T(8,128)S(1)}, ...), condition=%wide.region_30.31_spmd.clone, body=%wide.region_29.30_spmd.clone.sunk | while | flops 454852608 | bytes 20260232 | solution.py:354
  1408.4 22.5 %reshape.600 = f32[3,256,256]{2,1,0:T(8,128)} reshape(f32[3,64,4,64,4]{4,3,2,1,0:T(8,128)} %get-tuple-element.1269) | data formatting | bytes 1572864 | tf_op jit(solution)/shard_map/transpose(jvp())/reshape | solution.py:31
  1430.9 32.5 %multiply_bitcast_fusion.1 = (f32[3,128,2,128,2]{4,3,2,1,0:T(8,128)}, f32[3,128,2,128,2]{4,3,2,1,0:T(8,128)}) fusion(f32[128,128]{1,0:T(8,128)S(1)} %copy-done.221, f32[128,3,2,2]{3,2,0,1:T(2,128)S(1)} %copy-done.146, f32[128,3,2,2]{3,2,0,1:T(2,128)S(1)} %copy-done.148), kind=kLoop, calls=%fused_computation.79 | loop fusion | flops 393216 | bytes 1650688 | tf_op jit(solution)/shard_map/transpose(jvp(hiajb,ij->hiab))/transpose | solution.py:33
  1463.3 35.6 %reshape.586 = f32[3,256,256]{2,1,0:T(8,128)S(1)} reshape(f32[3,128,2,128,2]{4,3,2,1,0:T(8,128)} %get-tuple-element.1266) | data formatting | bytes 1572864 | tf_op jit(solution)/shard_map/transpose(jvp())/reshape | solution.py:31
  1500.1 36.2 %reshape.602 = f32[3,256,256]{2,1,0:T(8,128)} reshape(f32[3,128,2,128,2]{4,3,2,1,0:T(8,128)} %get-tuple-element.1267) | data formatting | bytes 1572864 | tf_op jit(solution)/shard_map/transpose(jvp())/reshape | solution.py:31
  1602.5 70.0 %all-reduce.71.cloned.1.call-done = f32[256,1536]{1,0:T(8,128)} async-done(((f32[256,1536]{1,0:T(8,128)}), f32[256,1536]{1,0:T(8,128)}) %all-reduce.71.cloned.1.call-update) | async-done | bytes 1572880 | tf_op jit(solution)/shard_map/psum | solution.py:376
  1676.1 26.5 %all-reduce.62 = (f32[1536]{0:T(1024)S(1)}, f32[1536]{0:T(1024)S(1)}) all-reduce(f32[1536]{0:T(1024)S(1)} %get-tuple-element.1102, f32[1536]{0:T(1024)S(1)} %copy-done.255), channel_id=5, replica_groups=mesh['seq'=2,'hid'=4,'wid'=4] {'seq','hid'}, use_global_device_ids=true, to_apply=%region_39.40.clone | all-reduce | flops 3072 | bytes 24576
  1709.6 47.9 %reduce-scatter.22.cloned.1.call-done = f32[192,384]{1,0:T(8,128)} async-done(((f32[1536,384]{1,0:T(8,128)}), f32[192,384]{1,0:T(8,128)}) %reduce-scatter.22.cloned.1.call-update) | async-done | bytes 294928 | tf_op jit(solution)/shard_map/reduce_scatter | solution.py:385
  1757.5 46.4 %reduce-scatter.20.cloned.1.call-done = f32[192,384]{1,0:T(8,128)} async-done(((f32[1536,384]{1,0:T(8,128)}), f32[192,384]{1,0:T(8,128)}) %reduce-scatter.20.cloned.1.call-update) | async-done | bytes 294928 | tf_op jit(solution)/shard_map/reduce_scatter | solution.py:384
  1803.9 46.6 %reduce-scatter.18.cloned.1.call-done = f32[192,384]{1,0:T(8,128)} async-done(((f32[1536,384]{1,0:T(8,128)}), f32[192,384]{1,0:T(8,128)}) %reduce-scatter.18.cloned.1.call-update) | async-done | bytes 294928 | tf_op jit(solution)/shard_map/reduce_scatter | solution.py:383
  1850.5 46.3 %reduce-scatter.26.cloned.1.call-done = f32[384,192]{0,1:T(8,128)} async-done(((f32[384,1536]{0,1:T(8,128)}), f32[384,192]{0,1:T(8,128)}) %reduce-scatter.26.cloned.1.call-update) | async-done | bytes 294928 | tf_op jit(solution)/shard_map/reduce_scatter | solution.py:388
  1896.8 46.6 %reduce-scatter.24.cloned.1.call-done = f32[192,384]{1,0:T(8,128)} async-done(((f32[1536,384]{1,0:T(8,128)}), f32[192,384]{1,0:T(8,128)}) %reduce-scatter.24.cloned.1.call-update) | async-done | bytes 294928 | tf_op jit(solution)/shard_map/reduce_scatter | solution.py:386
  (1317 shorter events, 1063.5 us)
Async XLA Ops:
  7.2 636.4 %all-reduce.67.cloned.1.call-start = ((), (), s32[]{:S(2)}) async-start(), calls=%async_computation.11 | async-start | bytes 3145728 | tf_op jit(solution)/shard_map/psum | solution.py:222
  574.3 116.5 %all-gather.6.cloned.1.call-start = ((), (), s32[]{:S(2)}) async-start(), calls=%async_computation.12 | async-start | bytes 3932160 | tf_op jit(solution)/shard_map/all_gather | solution.py:225
  647.6 114.1 %all-gather.8.cloned.1.call-start = ((), (), s32[]{:S(2)}) async-start(), calls=%async_computation.25 | async-start | bytes 3342336 | tf_op jit(solution)/shard_map/all_gather | solution.py:255
  648.3 312.8 %reduce-scatter.16.cloned.1.call-start = ((), (), s32[]{:S(2)}) async-start(), calls=%async_computation.14 | async-start | bytes 7864320 | tf_op jit(solution)/shard_map/reduce_scatter | solution.py:286
  892.3 150.8 %all-reduce.69.cloned.1.call-start = ((), (), s32[]{:S(2)}) async-start(), calls=%async_computation.15 | async-start | bytes 3145728 | tf_op jit(solution)/shard_map/psum | solution.py:292
  961.2 630.8 %reduce-scatter.14.cloned.1.call-start = ((), (), s32[]{:S(2)}) async-start(), calls=%async_computation.13 | async-start | bytes 3342336 | tf_op jit(solution)/shard_map/reduce_scatter | solution.py:241
  1043.0 557.9 %reduce-scatter.34.cloned.1.call-start = ((), (), s32[]{:S(2)}) async-start(), calls=%async_computation.26 | async-start | bytes 884736
  1069.4 24.3 %collective-permute-start.3 = (f32[3,256,128]{2,1,0:T(8,128)}, f32[3,256,128]{2,1,0:T(8,128)}, u32[]{:S(2)}, u32[]{:S(2)}) collective-permute-start(f32[3,256,128]{2,1,0:T(8,128)} %convolution_add_fusion.51), channel_id=1, source_target_pairs={{4,0},{8,4},{12,8},{16,12},{20,16},{24,20},{28,24},{5,1},{9,5},{13... | collective-permute-start | bytes 1179656 | tf_op jit(solution)/shard_map/while/body/eval_jaxpr/ppermute | solution.py:18
  1074.5 19.2 collective-permute-start.2
  1096.3 23.3 %collective-permute-start.3 = (f32[3,256,128]{2,1,0:T(8,128)}, f32[3,256,128]{2,1,0:T(8,128)}, u32[]{:S(2)}, u32[]{:S(2)}) collective-permute-start(f32[3,256,128]{2,1,0:T(8,128)} %convolution_add_fusion.51), channel_id=1, source_target_pairs={{4,0},{8,4},{12,8},{16,12},{20,16},{24,20},{28,24},{5,1},{9,5},{13... | collective-permute-start | bytes 1179656 | tf_op jit(solution)/shard_map/while/body/eval_jaxpr/ppermute | solution.py:18
  1101.4 18.2 collective-permute-start.2
  1122.3 21.8 %collective-permute-start.3 = (f32[3,256,128]{2,1,0:T(8,128)}, f32[3,256,128]{2,1,0:T(8,128)}, u32[]{:S(2)}, u32[]{:S(2)}) collective-permute-start(f32[3,256,128]{2,1,0:T(8,128)} %convolution_add_fusion.51), channel_id=1, source_target_pairs={{4,0},{8,4},{12,8},{16,12},{20,16},{24,20},{28,24},{5,1},{9,5},{13... | collective-permute-start | bytes 1179656 | tf_op jit(solution)/shard_map/while/body/eval_jaxpr/ppermute | solution.py:18
  1127.4 16.7 collective-permute-start.2
  1146.7 22.0 %collective-permute-start.3 = (f32[3,256,128]{2,1,0:T(8,128)}, f32[3,256,128]{2,1,0:T(8,128)}, u32[]{:S(2)}, u32[]{:S(2)}) collective-permute-start(f32[3,256,128]{2,1,0:T(8,128)} %convolution_add_fusion.51), channel_id=1, source_target_pairs={{4,0},{8,4},{12,8},{16,12},{20,16},{24,20},{28,24},{5,1},{9,5},{13... | collective-permute-start | bytes 1179656 | tf_op jit(solution)/shard_map/while/body/eval_jaxpr/ppermute | solution.py:18
  1151.8 16.9 collective-permute-start.2
  1564.7 107.8 %all-reduce.71.cloned.1.call-start = ((), (), s32[]{:S(2)}) async-start(), calls=%async_computation.16 | async-start | bytes 3145728 | tf_op jit(solution)/shard_map/psum | solution.py:376
  1567.8 138.2 %reduce-scatter.30.cloned.1.call-start = ((), (), s32[]{:S(2)}) async-start(), calls=%async_computation.23 | async-start | bytes 2359296 | tf_op jit(solution)/shard_map/reduce_scatter | solution.py:392
  1574.6 131.3 %reduce-scatter.28.cloned.1.call-start = ((), (), s32[]{:S(2)}) async-start(), calls=%async_computation.22 | async-start | bytes 2359296 | tf_op jit(solution)/shard_map/reduce_scatter | solution.py:391
  1575.2 134.4 %reduce-scatter.32.cloned.1.call-start = ((), (), s32[]{:S(2)}) async-start(), calls=%async_computation.24 | async-start | bytes 2359296 | tf_op jit(solution)/shard_map/reduce_scatter | solution.py:393
  1576.0 181.5 %reduce-scatter.22.cloned.1.call-start = ((), (), s32[]{:S(2)}) async-start(), calls=%async_computation.19 | async-start | bytes 2654208 | tf_op jit(solution)/shard_map/reduce_scatter | solution.py:385
  1578.2 225.7 %reduce-scatter.20.cloned.1.call-start = ((), (), s32[]{:S(2)}) async-start(), calls=%async_computation.18 | async-start | bytes 2654208 | tf_op jit(solution)/shard_map/reduce_scatter | solution.py:384
  1580.4 270.1 %reduce-scatter.18.cloned.1.call-start = ((), (), s32[]{:S(2)}) async-start(), calls=%async_computation.17 | async-start | bytes 2654208 | tf_op jit(solution)/shard_map/reduce_scatter | solution.py:383
  1583.5 313.3 %reduce-scatter.26.cloned.1.call-start = ((), (), s32[]{:S(2)}) async-start(), calls=%async_computation.21 | async-start | bytes 2654208 | tf_op jit(solution)/shard_map/reduce_scatter | solution.py:388
  1587.8 355.6 %reduce-scatter.24.cloned.1.call-start = ((), (), s32[]{:S(2)}) async-start(), calls=%async_computation.20 | async-start | bytes 2654208 | tf_op jit(solution)/shard_map/reduce_scatter | solution.py:386
  (301 other events, 3205.5 us)
Sparse Core Ops, SparseCore 0:
  574.4 69.1 all-reduce.66
  647.7 43.0 all-gather.5
  693.6 68.0 all-gather.7
  892.4 68.6 reduce-scatter.15
  963.4 69.0 all-reduce.68
  1043.1 156.9 reduce-scatter.13
  1564.8 36.0 reduce-scatter.33
  1603.3 69.1 all-reduce.70
  1675.3 8.0 reduce-scatter.29
  1686.2 10.2 reduce-scatter.27
  1699.3 10.2 reduce-scatter.31
  1713.7 43.6 reduce-scatter.21
  1761.4 42.4 reduce-scatter.19
  1808.0 42.4 reduce-scatter.17
  1854.3 42.4 reduce-scatter.25
  1900.9 42.4 reduce-scatter.23
where the time goes:
time: 1960 us; the launch traced here: 1950 us
  waiting for transfers between devices  599 us (31%)
  local copies, waits for them, and re-layouts  575 us (29%)
  matrix products  431 us (22%)
  other arithmetic  166 us (8%)
  blocking collectives  70.1 us (4%)
  loops' own time  46.1 us (2%)
  starting transfers between devices  44.3 us (2%)
    reshape x35, local copies, waits for them, and re-layouts, unit_lower_inverse(): shaped = matrix.reshape(heads_n, count, 2 * span, count, 2 * span)  372 us
    dot_general x14, matrix products, unit_lower_inverse(): jnp.einsum('hiajb,ij->hiab', shaped, picker, precision=highest)  108 us
    transpose x7, other arithmetic, unit_lower_inverse(): jnp.einsum('hiajb,ij->hiab', shaped, picker, precision=highest)  76.9 us
    psum x1, waiting for transfers between devices, body(): grad_act = lax.psum(grad_act, 'wid')  70 us
    reduce_scatter x1, waiting for transfers between devices, body(): lax.psum_scatter(jnp.einsum('tf,cf->tc', rows_of, gate_up, preferred_elem...  64.4 us
    all_gather x1, waiting for transfers between devices, body(): shard_rows = lax.all_gather(dy_blocks, ('hid', 'wid'), axis=0, tiled=True)  64 us
    ppermute x16, waiting for transfers between devices, shifted(): return lax.ppermute(array, axis, pairs)  57.4 us
    psum x1, waiting for transfers between devices, body(): mixed = residual + lax.psum(attn_part, 'wid')  57.1 us
  transfers between devices with their start and end apart: 32, of which 20 were waited for; matrix products, arithmetic and copies ran while one was open for 28% of the time, Pallas kernels for 0%

commit v1 on v0

v1 whole, which is shorter than its diff:
```python
import functools

import jax
import jax.numpy as jnp
from jax import lax
from jax.experimental import pallas as pl
from jax.experimental.pallas import tpu as pltpu
from jax.sharding import PartitionSpec as P

HDIM = 128
LEAST = 1024

eps_norm = 1e-06
neg_big = -1e30
BF = jnp.bfloat16
F32 = jnp.float32
VMEM_LIMIT = 60 * 1024 * 1024


def dot(a, b, ca, cb):
    return lax.dot_general(a, b, (((ca,), (cb,)), ((), ())), preferred_element_type=F32)


def split(a):
    hi = a.astype(BF)
    return hi, (a - hi.astype(F32)).astype(BF)


def dot3(a, b, ca, cb):
    return dot(a[0], b[0], ca, cb) + (dot(a[0], b[1], ca, cb) + dot(a[1], b[0], ca, cb))


def dot1(a, b, ca, cb):
    return dot(a.astype(BF), b.astype(BF), ca, cb)


def iotas(n):
    rows = lax.broadcasted_iota(jnp.int32, (n, n), 0)
    cols = lax.broadcasted_iota(jnp.int32, (n, n), 1)
    return rows, cols


def head_cols(h):
    return slice(h * HDIM, (h + 1) * HDIM)


def house_terms(raw, strength, heads, h):
    inv = lax.rsqrt(jnp.sum(raw * raw, -1, keepdims=True) + eps_norm)
    lane = lax.broadcasted_iota(jnp.int32, strength.shape, 1)
    c = jnp.sum(jnp.where(lane == h, strength, 0.0), 1, keepdims=True)
    root = jnp.sqrt(2.0 / (1.0 + jnp.exp(-c)))
    return inv, root


def path_fwd_kernel(heads, q_ref, k_ref, r_ref, c_ref, qt_ref, kt_ref, near_ref, p_ref,
                    u_ref, inv_ref, psi_ref, x_ref, y_ref):
    n = q_ref.shape[0]
    rows, cols = iotas(n)
    strength = c_ref[...]
    us, us2, lows, invs = [], [], [], []
    for h in range(heads):
        raw = r_ref[:, head_cols(h)]
        inv, root = house_terms(raw, strength, heads, h)
        u = raw * (inv * root)
        u_ref[:, head_cols(h)] = u
        u2 = split(u)
        low = jnp.where(rows > cols, dot3(u2, u2, 1, 1), 0.0)
        us.append(u)
        us2.append(u2)
        lows.append(low)
        first = jnp.where(rows == cols, 1.0, 0.0) - jnp.where(rows // 2 == cols // 2, low, 0.0)
        invs.append(first)
    span = 2
    while span < n:
        pick = (rows // (2 * span) == cols // (2 * span)) & (rows // span != cols // span)
        halves = [split(m) for m in invs]
        mids = [dot3(split(jnp.where(pick, lows[h], 0.0)), halves[h], 1, 0) for h in range(heads)]
        invs = [invs[h] - dot3(halves[h], split(mids[h]), 1, 0) for h in range(heads)]
        span = span * 2
    for h in range(heads):
        inv_ref[h] = invs[h]
        kin = split(invs[h])
        q = q_ref[:, head_cols(h)]
        k = k_ref[:, head_cols(h)]
        q2, k2, u2 = split(q), split(k), us2[h]
        a = jnp.where(rows > cols, dot3(u2, k2, 1, 1), 0.0)
        aq = jnp.where(rows < cols, dot3(k2, u2, 1, 1), 0.0)
        fq = jnp.where(rows >= cols, dot3(q2, u2, 1, 1), 0.0)
        fq2 = split(fq)
        x = dot3(kin, u2, 1, 0)
        y = dot3(kin, u2, 0, 0)
        psi = dot3(kin, split(a), 1, 0)
        x2 = split(x)
        x_ref[:, head_cols(h)] = x
        y_ref[:, head_cols(h)] = y
        psi_ref[h] = psi
        qt_ref[:, head_cols(h)] = (q - dot3(fq2, x2, 1, 0)).astype(BF)
        kt_ref[:, head_cols(h)] = (k - dot3(split(aq), split(y), 1, 0)).astype(BF)
        near_ref[h] = dot3(q2, k2, 1, 1) - dot3(fq2, split(psi), 1, 0)
        er, ec = iotas(HDIM)
        p_ref[h] = jnp.where(er == ec, 1.0, 0.0) - dot3(u2, x2, 0, 0)


def path_fwd(q, k, r, c, heads):
    n, width = q.shape
    flat = jax.ShapeDtypeStruct((n, width), F32)
    low = jax.ShapeDtypeStruct((n, width), BF)
    square = jax.ShapeDtypeStruct((heads, n, n), F32)
    return pl.pallas_call(
        functools.partial(path_fwd_kernel, heads),
        out_shape=(low, low, square, jax.ShapeDtypeStruct((heads, HDIM, HDIM), F32),
                   flat, square, square, flat, flat),
        compiler_params=pltpu.CompilerParams(vmem_limit_bytes=VMEM_LIMIT),
        name="path_fwd",
    )(q, k, r, c)


def doc_of(pos, len_ref):
    total = len_ref[0]
    doc = (pos >= total).astype(jnp.int32)
    for i in range(1, len_ref.shape[0]):
        total = total + len_ref[i]
        doc = doc + (pos >= total).astype(jnp.int32)
    return doc


def chain_slot(r, m):
    return r * (r - 1) // 2 + m


def attn_fwd_kernel(heads, hops, len_ref, row_ref, qt_ref, near_ref, v_ref, fk_ref, fv_ref, fp_ref,
                    o_ref, p_ref, chain_ref, s_ref):
    n = qt_ref.shape[0]
    scale = HDIM ** (-0.5)
    row = row_ref[0]
    rows, cols = iotas(n)
    own = doc_of(row * n + rows, len_ref)
    near_ok = (rows >= cols) & (own == doc_of(row * n + cols, len_ref))
    for h in range(heads):
        cs = head_cols(h)
        q = qt_ref[:, cs]
        s = jnp.where(near_ok, near_ref[h] * scale, neg_big)
        s_ref[h, 0] = s
        top = jnp.max(s, 1, keepdims=True)
        for r in range(1, hops + 1):
            keys = fk_ref[r - 1, :, cs]
            chain_ref[chain_slot(r, 0), :, cs] = keys
            for m in range(1, r):
                ph, plo = split(fp_ref[r - m - 1, h])
                keys = (dot(keys, ph, 1, 1) + dot(keys, plo, 1, 1)).astype(BF)
                chain_ref[chain_slot(r, m), :, cs] = keys
            source = row - r
            docs = jnp.where(source >= 0, doc_of(source * n + cols, len_ref), -1)
            s = jnp.where(own == docs, dot(q, keys, 1, 1) * scale, neg_big)
            s_ref[h, r] = s
            top = jnp.maximum(top, jnp.max(s, 1, keepdims=True))
        total = jnp.zeros((n, 1), F32)
        for r in range(hops + 1):
            e = jnp.exp(s_ref[h, r] - top)
            s_ref[h, r] = e
            total = total + jnp.sum(e, 1, keepdims=True)
        recip = 1.0 / total
        out = jnp.zeros((n, HDIM), F32)
        for r in range(hops + 1):
            p = (s_ref[h, r] * recip).astype(BF)
            p_ref[r, h] = p
            vals = v_ref[:, cs] if r == 0 else fv_ref[r - 1, :, cs]
            out = out + dot(p, vals, 1, 0)
        o_ref[:, cs] = out.astype(BF)


def attn_fwd(lengths, my_row, qt, near, v, far_k, far_v, far_p, heads, hops):
    n, width = qt.shape
    slots = hops * (hops + 1) // 2
    smem = pl.BlockSpec(memory_space=pltpu.SMEM)
    vmem = pl.BlockSpec(memory_space=pltpu.VMEM)
    return pl.pallas_call(
        functools.partial(attn_fwd_kernel, heads, hops),
        in_specs=[smem, smem] + [vmem] * 6,
        out_shape=(
            jax.ShapeDtypeStruct((n, width), BF),
            jax.ShapeDtypeStruct((hops + 1, heads, n, n), BF),
            jax.ShapeDtypeStruct((slots, n, width), BF),
        ),
        scratch_shapes=[pltpu.VMEM((heads, hops + 1, n, n), F32)],
        compiler_params=pltpu.CompilerParams(vmem_limit_bytes=VMEM_LIMIT),
        name="attn_fwd",
    )(lengths, my_row, qt, near, v, far_k, far_v, far_p)


def attn_bwd_kernel(heads, hops, p_ref, go_ref, qt_ref, v_ref, fv_ref, fp_ref, chain_ref,
                    gqt_ref, gnear_ref, gv_ref, sendk_ref, sendv_ref, sendp_ref, dp_ref):
    n = qt_ref.shape[0]
    scale = HDIM ** (-0.5)
    for h in range(heads):
        cs = head_cols(h)
        go = go_ref[:, cs]
        q = qt_ref[:, cs]
        delta = jnp.zeros((n, 1), F32)
        for r in range(hops + 1):
            vals = v_ref[:, cs] if r == 0 else fv_ref[r - 1, :, cs]
            dp = dot(go, vals, 1, 1)
            dp_ref[r] = dp
            delta = delta + jnp.sum(p_ref[r, h].astype(F32) * dp, 1, keepdims=True)
            gv = dot(p_ref[r, h], go, 0, 0)
            if r == 0:
                gv_ref[:, cs] = gv
            else:
                sendv_ref[r - 1, :, cs] = gv.astype(BF)
        gnear_ref[h] = p_ref[0, h].astype(F32) * (dp_ref[0] - delta) * scale
        gq = jnp.zeros((n, HDIM), F32)
        gps = [jnp.zeros((HDIM, HDIM), F32) for _ in range(hops - 1)]
        for r in range(1, hops + 1):
            gs = (p_ref[r, h].astype(F32) * (dp_ref[r] - delta) * scale).astype(BF)
            gq = gq + dot(gs, chain_ref[chain_slot(r, r - 1), :, cs], 1, 0)
            gk = dot(gs, q, 0, 0)
            for m in range(r - 1, 0, -1):
                back = r - m - 1
                gkb = gk.astype(BF)
                gps[back] = gps[back] + dot(gkb, chain_ref[chain_slot(r, m - 1), :, cs], 0, 0)
                gk = dot(gkb, fp_ref[back, h].astype(BF), 1, 0)
            sendk_ref[r - 1, :, cs] = gk.astype(BF)
        gqt_ref[:, cs] = gq
        for i in range(hops - 1):
            sendp_ref[i, h] = gps[i].astype(BF)


def attn_bwd(p, go, qt, v, far_v, far_p, chain, heads, hops):
    n, width = qt.shape
    return pl.pallas_call(
        functools.partial(attn_bwd_kernel, heads, hops),
        out_shape=(
            jax.ShapeDtypeStruct((n, width), F32),
            jax.ShapeDtypeStruct((heads, n, n), F32),
            jax.ShapeDtypeStruct((n, width), F32),
            jax.ShapeDtypeStruct((hops, n, width), BF),
            jax.ShapeDtypeStruct((hops, n, width), BF),
            jax.ShapeDtypeStruct((hops - 1, heads, HDIM, HDIM), BF),
        ),
        scratch_shapes=[pltpu.VMEM((hops + 1, n, n), F32)],
        compiler_params=pltpu.CompilerParams(vmem_limit_bytes=VMEM_LIMIT),
        name="attn_bwd",
    )(p, go, qt, v, far_v, far_p, chain)


def path_bwd_kernel(heads, q_ref, k_ref, r_ref, c_ref, u_ref, inv_ref, psi_ref, x_ref, y_ref,
                    gqt_ref, gkt_ref, gnear_ref, gp_ref, gq_ref, gk_ref, gr_ref, gc_ref):
    n = q_ref.shape[0]
    rows, cols = iotas(n)
    strength = c_ref[...]
    lane = lax.broadcasted_iota(jnp.int32, strength.shape, 1)
    gc_all = jnp.zeros(strength.shape, F32)
    for h in range(heads):
        cs = head_cols(h)
        q, k, u = q_ref[:, cs], k_ref[:, cs], u_ref[:, cs]
        qb, kb, ub = q.astype(BF), k.astype(BF), u.astype(BF)
        kin = inv_ref[h].astype(BF)
        psi = psi_ref[h].astype(BF)
        x, y = x_ref[:, cs].astype(BF), y_ref[:, cs].astype(BF)
        gqt, gkt = gqt_ref[:, cs], gkt_ref[:, cs]
        gqtb, gktb = gqt.astype(BF), gkt.astype(BF)
        gs = gnear_ref[h]
        gsb = gs.astype(BF)
        gst = gs.T.astype(BF)
        gp = gp_ref[h].astype(BF)
        f = jnp.where(rows <= cols, dot(ub, qb, 1, 1), 0.0).astype(BF)
        fq = jnp.where(rows >= cols, dot(qb, ub, 1, 1), 0.0).astype(BF)
        a = jnp.where(rows > cols, dot(ub, kb, 1, 1), 0.0).astype(BF)
        gx = -(dot(f, gqtb, 1, 0) + dot(ub, gp, 1, 0))
        gy = -dot(a, gktb, 1, 0)
        phiq = dot(fq, kin, 1, 0).astype(BF)
        back = dot(gst, phiq, 1, 0)
        backb = back.astype(BF)
        gfq = jnp.where(rows >= cols, -(dot(gqtb, x, 1, 1) + dot(gsb, psi, 1, 1)), 0.0)
        gaq = jnp.where(rows < cols, -(dot(gktb, y, 1, 1) + back), 0.0)
        kgx = dot(kin, gx.astype(BF), 0, 0)
        kgy = dot(kin, gy.astype(BF), 1, 0)
        zt = dot(x, kgx.astype(BF), 1, 1) + dot(kgy.astype(BF), y, 1, 1) - dot(psi, backb, 1, 0)
        glt = jnp.where(rows < cols, -zt, 0.0)
        sym = (glt + glt.T).astype(BF)
        gfqb, gaqb = gfq.astype(BF), gaq.astype(BF)
        gu = (kgx + kgy - dot(x, gp, 1, 1) + dot(gfq.T.astype(BF), qb, 1, 0)
              + dot(gaq.T.astype(BF), kb, 1, 0) + dot(sym, ub, 1, 0))
        gq_ref[:, cs] = (gqt + dot(gsb, kb, 1, 0) + dot(gfqb, ub, 1, 0)).astype(BF)
        gk_ref[:, cs] = (gkt + dot(gst, qb, 1, 0) + dot(gaqb, ub, 1, 0)).astype(BF)
        raw = r_ref[:, cs]
        inv, root = house_terms(raw, strength, heads, h)
        gc = jnp.sum(gu * u, 1, keepdims=True) * (1.0 - 0.5 * root * root) * 0.5
        gun = gu * root
        un = raw * inv
        gr = inv * (gun - un * jnp.sum(gun * un, 1, keepdims=True))
        gr_ref[:, cs] = gr.astype(BF)
        gc_all = jnp.where(lane == h, gc, gc_all)
    gc_ref[...] = gc_all.astype(BF)


def path_bwd(q, k, r, c, saved, gqt, gkt, gnear, gp, heads):
    n, width = q.shape
    low = jax.ShapeDtypeStruct((n, width), BF)
    return pl.pallas_call(
        functools.partial(path_bwd_kernel, heads),
        out_shape=(low, low, low, jax.ShapeDtypeStruct((n, heads), BF)),
        compiler_params=pltpu.CompilerParams(vmem_limit_bytes=VMEM_LIMIT),
        name="path_bwd",
    )(q, k, r, c, *saved, gqt, gkt, gnear, gp)


def shifted(array, axis, by):
    peers = lax.axis_size(axis)
    pairs = [(i, i + by) for i in range(peers) if 0 <= i + by < peers]
    return lax.ppermute(array, axis, pairs)


def norm_rows(hidden_f):
    inverse = lax.rsqrt(jnp.mean(hidden_f * hidden_f, -1, keepdims=True) + eps_norm)
    return (hidden_f * inverse, inverse)


def norm_back(grad_out, normed, inverse, gain_vec):
    scaled_grad = grad_out * gain_vec
    grad_gain = jnp.sum(grad_out * normed, 0)
    grad_in = inverse * (scaled_grad - normed * jnp.mean(scaled_grad * normed, -1, keepdims=True))
    return (grad_in, grad_gain)


ROWS = ("seq", "hid")


def body(inputs, gain_attn, gain_ffn, w_query, w_key, w_value, w_house, w_beta, w_out,
         w_gate, w_up, w_down, lengths, cotangent):
    tok, col = inputs.shape
    row_devs = lax.axis_size(ROWS)
    my_row = lax.axis_index(ROWS)
    my_wid = lax.axis_index("wid")
    wid_n = lax.axis_size("wid")
    tokens_all = tok * row_devs
    most_len = max(LEAST, 2 * tokens_all // 5)
    hops = min((most_len - 2) // tok + 1, row_devs - 1)
    heads = w_query.shape[1] // HDIM
    ff = w_gate.shape[1]
    sub = tok // wid_n

    x_all = lax.all_gather(inputs, "wid", axis=1, tiled=True)
    gain_one = lax.all_gather(gain_attn, "wid", axis=0, tiled=True).astype(F32)
    gain_two = lax.all_gather(gain_ffn, "wid", axis=0, tiled=True).astype(F32)
    dy_all = lax.all_gather(cotangent, "wid", axis=1, tiled=True)
    w_gu = lax.all_gather(jnp.concatenate([w_gate, w_up], 1), "hid", axis=0)
    w_dn = lax.all_gather(w_down, "hid", axis=0)
    model = x_all.shape[1]

    residual = x_all.astype(F32)
    normed_one, inverse_one = norm_rows(residual)
    act = (normed_one * gain_one).astype(BF)

    def project(weight):
        return jnp.dot(act, weight, preferred_element_type=F32)

    q, k, r, c = project(w_query), project(w_key), project(w_house), project(w_beta)
    v = project(w_value).astype(BF)
    far_v = jnp.stack([shifted(v, ROWS, i) for i in range(1, hops + 1)])
    qt, kt, near, prod, *saved = path_fwd(q, k, r, c, heads)
    far_k = jnp.stack([shifted(kt, ROWS, i) for i in range(1, hops + 1)])
    far_p = jnp.stack([shifted(prod, ROWS, i) for i in range(1, hops)])
    row_arr = jnp.full((1,), my_row, jnp.int32)
    attended, probs, chain = attn_fwd(lengths, row_arr, qt, near, v, far_k, far_v, far_p, heads, hops)

    attn_part = jnp.dot(attended, w_out, preferred_element_type=F32).astype(BF)
    attn_rows = lax.psum_scatter(attn_part, "wid", scatter_dimension=0, tiled=True)
    x_rows = lax.dynamic_slice_in_dim(x_all, my_wid * sub, sub, 0).astype(F32)
    dy_rows = lax.dynamic_slice_in_dim(dy_all, my_wid * sub, sub, 0).astype(F32)
    mixed = x_rows + attn_rows.astype(F32)
    normed_two, inverse_two = norm_rows(mixed)
    inner = lax.all_gather((normed_two * gain_two).astype(BF), "wid", axis=0, tiled=True)

    pre = jnp.einsum("tc,hcf->htf", inner, w_gu, preferred_element_type=F32)
    gate, up = pre[:, :, :ff], pre[:, :, ff:]
    sig = jax.nn.sigmoid(gate)
    hidden = (gate * sig * up).astype(BF)
    ffn_part = jnp.einsum("htf,hfc->tc", hidden, w_dn, preferred_element_type=F32)
    ffn_part = (ffn_part + attn_part.astype(F32)).astype(BF)
    ffn_cols = lax.psum_scatter(ffn_part, "wid", scatter_dimension=1, tiled=True)
    output = (inputs.astype(F32) + ffn_cols.astype(F32)).astype(BF)

    g_hidden = jnp.einsum("tc,hfc->htf", dy_all, w_dn, preferred_element_type=F32)
    g_gate = g_hidden * up * sig * (1.0 + gate * (1.0 - sig))
    g_up = g_hidden * gate * sig
    g_pre = jnp.concatenate([g_gate, g_up], 2).astype(BF)
    g_inner = jnp.einsum("htf,hcf->tc", g_pre, w_gu, preferred_element_type=F32).astype(BF)
    g_inner = lax.psum_scatter(g_inner, "wid", scatter_dimension=0, tiled=True).astype(F32)
    g_mixed_n, g_gain_two = norm_back(g_inner, normed_two, inverse_two, gain_two)
    g_z = lax.all_gather((dy_rows + g_mixed_n).astype(BF), "wid", axis=0, tiled=True)

    d_gu = jnp.einsum("tc,htf->hcf", inner, g_pre, preferred_element_type=F32).astype(BF)
    d_dn = jnp.einsum("htf,tc->hfc", hidden, dy_all, preferred_element_type=F32).astype(BF)
    d_gu = lax.psum_scatter(d_gu, "seq", scatter_dimension=1, tiled=True)
    d_gu = lax.psum_scatter(d_gu, "hid", scatter_dimension=0)
    d_dn = lax.psum_scatter(d_dn, "seq", scatter_dimension=2, tiled=True)
    d_dn = lax.psum_scatter(d_dn, "hid", scatter_dimension=0)

    g_attn = jnp.einsum("tc,ic->ti", g_z, w_out, preferred_element_type=F32).astype(BF)
    d_out = jnp.einsum("ti,tc->ic", attended, g_z, preferred_element_type=F32).astype(BF)
    g_qt, g_near, gv, send_k, send_v, send_p = attn_bwd(probs, g_attn, qt, v, far_v, far_p, chain, heads, hops)
    g_kt = sum(shifted(send_k[i - 1], ROWS, -i).astype(F32) for i in range(1, hops + 1))
    gv = gv + sum(shifted(send_v[i - 1], ROWS, -i).astype(F32) for i in range(1, hops + 1))
    g_prod = sum(shifted(send_p[i - 1], ROWS, -i).astype(F32) for i in range(1, hops))
    g_q, g_k, g_r, g_c = path_bwd(q, k, r, c, saved, g_qt, g_kt, g_near, g_prod, heads)
    g_v = gv.astype(BF)

    def weight_grad(grad_low):
        return jnp.einsum("tc,ti->ci", act, grad_low, preferred_element_type=F32).astype(BF)

    def input_grad(grad_low, weight):
        return jnp.einsum("ti,ci->tc", grad_low, weight, preferred_element_type=F32)

    g_act = (input_grad(g_q, w_query) + input_grad(g_k, w_key) + input_grad(g_v, w_value)
             + input_grad(g_r, w_house) + input_grad(g_c, w_beta))
    g_act = lax.psum_scatter(g_act.astype(BF), "wid", scatter_dimension=0, tiled=True).astype(F32)
    normed_rows = lax.dynamic_slice_in_dim(normed_one, my_wid * sub, sub, 0)
    inverse_rows = lax.dynamic_slice_in_dim(inverse_one, my_wid * sub, sub, 0)
    g_resid, g_gain_one = norm_back(g_act, normed_rows, inverse_rows, gain_one)
    d_rows = dy_rows + g_mixed_n + g_resid
    d_inputs = lax.all_to_all(d_rows, "wid", split_axis=1, concat_axis=0, tiled=True)

    def scatter(x, dim):
        return lax.psum_scatter(x, ROWS, scatter_dimension=dim, tiled=True)

    gains = lax.psum(jnp.stack([g_gain_one, g_gain_two]), "wid")
    gains = scatter(gains, 1)
    return (
        output,
        d_inputs,
        gains[0],
        gains[1],
        scatter(weight_grad(g_q), 0).astype(F32),
        scatter(weight_grad(g_k), 0).astype(F32),
        scatter(weight_grad(g_v), 0).astype(F32),
        scatter(weight_grad(g_r), 0).astype(F32),
        scatter(weight_grad(g_c), 0).astype(F32),
        scatter(d_out, 1).astype(F32),
        d_gu[:, :ff].astype(F32),
        d_gu[:, ff:].astype(F32),
        d_dn.astype(F32),
    )


def solution(mesh):
    in_specs = (
        P(("seq", "hid"), "wid"), P("wid"), P("wid"),
        P(None, "wid"), P(None, "wid"), P(None, "wid"), P(None, "wid"), P(None, "wid"),
        P("wid", None), P(None, ("hid", "wid")), P(None, ("hid", "wid")), P(("hid", "wid"), None),
        P(), P(("seq", "hid"), "wid"),
    )
    out_specs = (
        P(("seq", "hid"), "wid"), P(("seq", "hid"), "wid"), P(("seq", "hid")), P(("seq", "hid")),
        P(("seq", "hid"), "wid"), P(("seq", "hid"), "wid"), P(("seq", "hid"), "wid"),
        P(("seq", "hid"), "wid"), P(("seq", "hid"), "wid"), P("wid", ("seq", "hid")),
        P("seq", ("hid", "wid")), P("seq", ("hid", "wid")), P(("hid", "wid"), "seq"),
    )
    return jax.shard_map(body, mesh=mesh, in_specs=in_specs, out_specs=out_specs, check_vma=False)
```

time: 1960 us -> 799 us (0.41)
  local copies, waits for them, and re-layouts: 575 us -> 21.3 us
  matrix products: 431 us -> 48.8 us
  other arithmetic: 166 us -> 31 us
  waiting for transfers between devices: 599 us -> 470 us
  loops' own time: 46.1 us -> 0 us
  blocking collectives: 70.1 us -> 112 us
  Pallas kernels: 0 us -> 36.9 us
    dot_general x238 -> x24, matrix products: 429 us -> 48.8 us  [the longest x5 7.32 us: weight_grad(): jnp.einsum('tc,ti->ci', act, grad_low, preferred_element_type=F32)]
    reshape x41 -> x0, local copies, waits for them, and re-layouts: 377 us -> none  [the longest x35 372 us: unit_lower_inverse(): shaped = matrix.reshape(heads_n, count, 2 * span, count, 2 * span)]
    unnamed x17 -> x22, waiting for transfers between devices: 9.22 us -> 176 us
    psum x3 -> x0, waiting for transfers between devices: 127 us -> none  [the longest x1 70 us: body(): grad_act = lax.psum(grad_act, 'wid')]
    transpose x7 -> x0, other arithmetic: 76.9 us -> none  [unit_lower_inverse(): jnp.einsum('hiajb,ij->hiab', shaped, picker, precision=highest)]
    reduce_scatter x10, waiting for transfers between devices: 302 us -> 231 us  [the longest x5 181 us: scatter(): return lax.psum_scatter(x, ROWS, scatter_dimension=dim, tiled=True)]
    all_gather x3 -> x6, blocking collectives: 43.6 us -> 101 us  [the longest x1 20.7 us: body(): dy_all = lax.all_gather(cotangent, 'wid', axis=1, tiled=True)]
    ppermute x16 -> x22, waiting for transfers between devices: 57.4 us -> 8.91 us  [shifted(): return lax.ppermute(array, axis, pairs)]
  transfers between devices with their start and end apart: 32 -> 40, of which waited for: 20 -> 21; matrix products, arithmetic and copies ran while one was open for 28% -> 8% of each run, Pallas kernels for 0% -> 1%
where the time goes in v1:
time: 799 us; the launch traced here: 784 us
  waiting for transfers between devices  470 us (59%)
  blocking collectives  112 us (14%)
  matrix products  48.8 us (6%)
  starting transfers between devices  46.6 us (6%)
  Pallas kernels  36.9 us (5%)
  other arithmetic  31 us (4%)
  local copies, waits for them, and re-layouts  21.3 us (3%)
  between operations  16.4 us (2%)
    reduce_scatter x5, waiting for transfers between devices, scatter(): return lax.psum_scatter(x, ROWS, scatter_dimension=dim, tiled=True)  181 us
    unnamed x22, waiting for transfers between devices  176 us
    ppermute x22, starting transfers between devices, shifted(): return lax.ppermute(array, axis, pairs)  40.9 us
    all_gather x1, waiting for transfers between devices, body(): w_dn = lax.all_gather(w_down, 'hid', axis=0)  39.5 us
    reduce_scatter x1, waiting for transfers between devices, body(): lax.psum_scatter(g_inner, 'wid', scatter_dimension=0, tiled=True)  23.5 us
    all_gather x1, blocking collectives, body(): dy_all = lax.all_gather(cotangent, 'wid', axis=1, tiled=True)  20.7 us
    all_gather x1, blocking collectives, body(): lax.all_gather((normed_two * gain_two).astype(BF), 'wid', axis=0, tiled=T...  18.3 us
    all_gather x1, blocking collectives, body(): x_all = lax.all_gather(inputs, 'wid', axis=1, tiled=True)  18 us
  transfers between devices with their start and end apart: 40, of which 21 were waited for; matrix products, arithmetic and copies ran while one was open for 8% of the time, Pallas kernels for 1%

profile of v1, /device:TPU:0, one launch (start us, length us, event | category | flops | bytes accessed | tf_op | source)
XLA Modules:
  0.0 783.8 jit_solution(15574680208976330117)
XLA Ops:
  8.8 13.5 %all-gather.2 = bf16[4,1,384]{2,1,0:T(2,128)(2,1)S(1)} all-gather(bf16[1,1,384]{2,1,0:T(2,128)(2,1)S(1)} %reshape.75), channel_id=1, replica_groups=mesh['seq'=2,'hid'=4,'wid'=4] {'wid'}, dimensions={0}, use_global_device_ids=true | all-gather | bytes 3840 | tf_op jit(solution)/shard_map/all_gather | solution.py:344
  22.4 18.0 %all_gather.32 = bf16[256,1536]{1,0:T(8,128)(2,1)S(1)} all-gather(bf16[256,384]{1,0:T(8,128)(2,1)} %param.14), channel_id=1, replica_groups=mesh['seq'=2,'hid'=4,'wid'=4] {'wid'}, dimensions={1}, use_global_device_ids=true | all-gather | bytes 983040 | tf_op jit(solution)/shard_map/all_gather | solution.py:343
  46.0 11.4 %path_fwd.1 = (bf16[256,384]{1,0:T(8,128)(2,1)}, bf16[256,384]{1,0:T(8,128)(2,1)}, f32[3,256,256]{2,1,0:T(8,128)}, f32[3,128,128]{2,1,0:T(8,128)}, f32[256,384]{...) custom-call(f32[256,384]{1,0:T(8,128)} %fusion.28.q_ref, ...), custom_call_target="tpu_custom_call" | custom-call | tf_op jit(solution)/shard_map/path_fwd/pallas_call | solution.py:109
  89.6 8.5 %attn_fwd.1 = (bf16[256,384]{1,0:T(8,128)(2,1)}, bf16[5,3,256,256]{3,2,1,0:T(8,128)(2,1)}, bf16[10,256,384]{2,1,0:T(8,128)(2,1)}) custom-call(s32[3]{0:T(128)} %len_ref.1, s32[1]{0:T(128)} %bitcast.1.row_ref, bf16[256,384]{1,0:T(8,128)(2,1)} %get-tuple-element.35.qt_ref, f32[3,256,256]{2,1,0:T(8,128)} %get-tuple-element.36.near_ref, ...), custom_call_target="tpu_custom_call" | custom-call | tf_op jit(solution)/shard_map/attn_fwd/pallas_call | solution.py:177
  103.7 12.3 %all-gather.3 = bf16[4,1,384]{2,1,0:T(2,128)(2,1)S(1)} all-gather(bf16[1,1,384]{2,1,0:T(2,128)(2,1)S(1)} %reshape.77), channel_id=1, replica_groups=mesh['seq'=2,'hid'=4,'wid'=4] {'wid'}, dimensions={0}, use_global_device_ids=true | all-gather | bytes 3840 | tf_op jit(solution)/shard_map/all_gather | solution.py:345
  116.1 20.7 %all_gather.38 = bf16[256,1536]{1,0:T(8,128)(2,1)S(1)} all-gather(bf16[256,384]{1,0:T(8,128)(2,1)S(1)} %copy-done.33), channel_id=1, replica_groups=mesh['seq'=2,'hid'=4,'wid'=4] {'wid'}, dimensions={1}, use_global_device_ids=true | all-gather | bytes 983040 | tf_op jit(solution)/shard_map/all_gather | solution.py:346
  139.1 18.3 %all_gather.35 = bf16[256,1536]{1,0:T(8,128)(2,1)} all-gather(bf16[64,1536]{1,0:T(8,128)(2,1)S(1)} %multiply_convert_fusion.4), channel_id=1, replica_groups=mesh['seq'=2,'hid'=4,'wid'=4] {'wid'}, dimensions={0}, use_global_device_ids=true | all-gather | bytes 983040 | tf_op jit(solution)/shard_map/all_gather | solution.py:373
  157.4 16.0 %all-gather.7.cloned.1.call-done = bf16[6144,512]{1,0:T(8,128)(2,1)} async-done(((bf16[1536,512]{1,0:T(8,128)(2,1)}), bf16[6144,512]{1,0:T(8,128)(2,1)}) %all-gather.7.cloned.1.call-update) | async-done | bytes 6291472 | tf_op jit(solution)/shard_map/all_gather | solution.py:347
  179.5 39.5 %all-gather.9.cloned.1.call-done = bf16[1024,1536]{1,0:T(8,128)(2,1)} async-done(((bf16[256,1536]{1,0:T(8,128)(2,1)}), bf16[1024,1536]{1,0:T(8,128)(2,1)}) %all-gather.9.cloned.1.call-update) | async-done | bytes 3145744 | tf_op jit(solution)/shard_map/all_gather | solution.py:348
  226.6 23.5 %reduce-scatter.28.cloned.1.call-done = bf16[64,1536]{1,0:T(8,128)(2,1)} async-done(((bf16[256,1536]{1,0:T(8,128)(2,1)}), bf16[64,1536]{1,0:T(8,128)(2,1)}) %reduce-scatter.28.cloned.1.call-update) | async-done | bytes 196624 | tf_op jit(solution)/shard_map/reduce_scatter | solution.py:389
  252.5 17.9 %all_gather.39 = bf16[256,1536]{1,0:T(8,128)(2,1)S(1)} all-gather(bf16[64,1536]{1,0:T(8,128)(2,1)S(1)} %fusion.24), channel_id=1, replica_groups=mesh['seq'=2,'hid'=4,'wid'=4] {'wid'}, dimensions={0}, use_global_device_ids=true | all-gather | bytes 983040 | tf_op jit(solution)/shard_map/all_gather | solution.py:391
  272.5 9.7 %attn_bwd.1 = (f32[256,384]{1,0:T(8,128)}, f32[3,256,256]{2,1,0:T(8,128)}, f32[256,384]{1,0:T(8,128)}, bf16[4,256,384]{2,1,0:T(8,128)(2,1)}, bf16[4,256,384]{2,1...) custom-call(bf16[5,3,256,256]{3,2,1,0:T(8,128)(2,1)} %get-tuple-element.45.p_ref, ...), custom_call_target="tpu_custom_call" | custom-call | tf_op jit(solution)/shard_map/attn_bwd/pallas_call | solution.py:230
  364.1 17.9 %reduce-scatter.42.cloned.1.call-done = bf16[4,768,512]{1,2,0:T(8,128)(2,1)} async-done(((bf16[4,1536,512]{1,2,0:T(8,128)(2,1)}), bf16[4,768,512]{1,2,0:T(8,128)(2,1)}) %reduce-scatter.42.cloned.1.call-update) | async-done | bytes 3145744 | tf_op jit(solution)/shard_map/reduce_scatter | solution.py:395
  389.9 25.6 %reduce-scatter.46.cloned.1.call-done = bf16[384,256]{1,0:T(8,128)(2,1)} async-done(((bf16[1536,256]{1,0:T(8,128)(2,1)}), bf16[384,256]{1,0:T(8,128)(2,1)}) %reduce-scatter.46.cloned.1.call-update) | async-done | bytes 196624
  417.3 34.1 %reduce-scatter.48.cloned.1.call-done = bf16[192,3]{1,0:T(8,128)(2,1)} async-done(((bf16[1536,3]{1,0:T(8,128)(2,1)}), bf16[192,3]{1,0:T(8,128)(2,1)}) %reduce-scatter.48.cloned.1.call-update) | async-done | bytes 1168
  452.9 38.5 %reduce-scatter.40.cloned.1.call-done = bf16[384,192]{0,1:T(8,128)(2,1)} async-done(((bf16[384,1536]{0,1:T(8,128)(2,1)}), bf16[384,192]{0,1:T(8,128)(2,1)}) %reduce-scatter.40.cloned.1.call-update) | async-done | bytes 147472 | tf_op jit(solution)/shard_map/reduce_scatter | solution.py:425
  493.1 37.4 %reduce-scatter.50.cloned.1.call-done = f32[192,2]{1,0:T(8,128)} async-done(((f32[1536,2]{1,0:T(8,128)}), f32[192,2]{1,0:T(8,128)}) %reduce-scatter.50.cloned.1.call-update) | async-done | bytes 1552
  531.5 11.7 %psum.8 = f32[2,192]{1,0:T(2,128)S(1)} all-reduce(f32[2,192]{1,0:T(2,128)S(1)} %copy.60), channel_id=1, replica_groups=mesh['seq'=2,'hid'=4,'wid'=4] {'wid'}, use_global_device_ids=true, to_apply=%region_10.0 | all-reduce | flops 384 | bytes 3072 | tf_op jit(solution)/shard_map/psum | solution.py:427
  543.7 27.0 %reduce-scatter.32.cloned.1.call-done = bf16[192,384]{1,0:T(8,128)(2,1)} async-done(((bf16[1536,384]{1,0:T(8,128)(2,1)}), bf16[192,384]{1,0:T(8,128)(2,1)}) %reduce-scatter.32.cloned.1.call-update) | async-done | bytes 147472 | tf_op jit(solution)/shard_map/reduce_scatter | solution.py:425
  572.4 38.4 %reduce-scatter.34.cloned.1.call-done = bf16[192,384]{1,0:T(8,128)(2,1)} async-done(((bf16[1536,384]{1,0:T(8,128)(2,1)}), bf16[192,384]{1,0:T(8,128)(2,1)}) %reduce-scatter.34.cloned.1.call-update) | async-done | bytes 147472 | tf_op jit(solution)/shard_map/reduce_scatter | solution.py:425
  612.4 38.6 %reduce-scatter.36.cloned.1.call-done = bf16[192,384]{1,0:T(8,128)(2,1)} async-done(((bf16[1536,384]{1,0:T(8,128)(2,1)}), bf16[192,384]{1,0:T(8,128)(2,1)}) %reduce-scatter.36.cloned.1.call-update) | async-done | bytes 147472 | tf_op jit(solution)/shard_map/reduce_scatter | solution.py:425
  652.6 38.4 %reduce-scatter.38.cloned.1.call-done = bf16[192,384]{1,0:T(8,128)(2,1)} async-done(((bf16[1536,384]{1,0:T(8,128)(2,1)}), bf16[192,384]{1,0:T(8,128)(2,1)}) %reduce-scatter.38.cloned.1.call-update) | async-done | bytes 147472 | tf_op jit(solution)/shard_map/reduce_scatter | solution.py:425
  692.7 32.4 %reduce-scatter.54.cloned.1.call-done = bf16[1,256,768]{2,1,0:T(8,128)(2,1)} async-done(((bf16[4,256,768]{2,1,0:T(8,128)(2,1)}), bf16[1,256,768]{2,1,0:T(8,128)(2,1)}) %reduce-scatter.54.cloned.1.call-update) | async-done | bytes 393232
  727.1 45.1 %reduce-scatter.52.cloned.1.call-done = bf16[1,768,512]{1,2,0:T(8,128)(2,1)} async-done(((bf16[4,768,512]{1,2,0:T(8,128)(2,1)}), bf16[1,768,512]{1,2,0:T(8,128)(2,1)}) %reduce-scatter.52.cloned.1.call-update) | async-done | bytes 786448
  (246 shorter events, 172.9 us)
Async XLA Ops:
  8.0 128.7 %reduce-scatter.26.cloned.1.call-start = ((), (), s32[]{:S(2)}) async-start(), calls=%async_computation.16 | async-start | bytes 983040 | tf_op jit(solution)/shard_map/reduce_scatter | solution.py:368
  64.4 23.0 %collective-permute-start = (bf16[256,384]{1,0:T(8,128)(2,1)}, bf16[256,384]{1,0:T(8,128)(2,1)S(1)}, u32[]{:S(2)}, u32[]{:S(2)}) collective-permute-start(bf16[256,384]{1,0:T(8,128)(2,1)} %get-tuple-element.37), channel_id=1, source_target_pairs={{0,4},{4,8},{8,12},{12,16},{16,20},{20,24},{24,28},{1,5},{5,9},{9,... | collective-permute-start | bytes 589832 | tf_op jit(solution)/shard_map/ppermute | solution.py:311
  100.6 72.9 %all-gather.7.cloned.1.call-start = ((), (), s32[]{:S(2)}) async-start(), calls=%async_computation.26 | async-start | bytes 7864320 | tf_op jit(solution)/shard_map/all_gather | solution.py:347
  103.1 115.9 %all-gather.9.cloned.1.call-start = ((), (), s32[]{:S(2)}) async-start(), calls=%async_computation.27 | async-start | bytes 3932160 | tf_op jit(solution)/shard_map/all_gather | solution.py:348
  103.7 146.5 %reduce-scatter.28.cloned.1.call-start = ((), (), s32[]{:S(2)}) async-start(), calls=%async_computation.17 | async-start | bytes 983040 | tf_op jit(solution)/shard_map/reduce_scatter | solution.py:389
  226.6 125.1 %reduce-scatter.30.cloned.1.call-start = ((), (), s32[]{:S(2)}) async-start(), calls=%async_computation.18 | async-start | bytes 983040 | tf_op jit(solution)/shard_map/reduce_scatter | solution.py:417
  283.7 19.3 %collective-permute-start.14 = (bf16[256,384]{1,0:T(8,128)(2,1)S(1)}, bf16[256,384]{1,0:T(8,128)(2,1)S(1)}, u32[]{:S(2)}, u32[]{:S(2)}) collective-permute-start(bf16[256,384]{1,0:T(8,128)(2,1)S(1)} %get-tuple-element.110), channel_id=1, source_target_pairs={{16,0},{20,4},{24,8},{28,12},{17,1},{21,5},{25,9},{29,13},{18,2},{... | collective-permute-start | bytes 589832 | tf_op jit(solution)/shard_map/ppermute | solution.py:311
  285.0 19.3 %collective-permute-start.13 = (bf16[256,384]{1,0:T(8,128)(2,1)S(1)}, bf16[256,384]{1,0:T(8,128)(2,1)S(1)}, u32[]{:S(2)}, u32[]{:S(2)}) collective-permute-start(bf16[256,384]{1,0:T(8,128)(2,1)S(1)} %get-tuple-element.111), channel_id=1, source_target_pairs={{12,0},{16,4},{20,8},{24,12},{28,16},{13,1},{17,5},{21,9},{25,13},... | collective-permute-start | bytes 589832 | tf_op jit(solution)/shard_map/ppermute | solution.py:311
  300.9 17.9 %collective-permute-start.21 = (bf16[256,384]{1,0:T(8,128)(2,1)}, bf16[256,384]{1,0:T(8,128)(2,1)}, u32[]{:S(2)}, u32[]{:S(2)}) collective-permute-start(bf16[256,384]{1,0:T(8,128)(2,1)} %get-tuple-element.106), channel_id=1, source_target_pairs={{16,0},{20,4},{24,8},{28,12},{17,1},{21,5},{25,9},{29,13},{18,2},{... | collective-permute-start | bytes 589832 | tf_op jit(solution)/shard_map/ppermute | solution.py:311
  303.0 15.9 %collective-permute-start.20 = (bf16[256,384]{1,0:T(8,128)(2,1)}, bf16[256,384]{1,0:T(8,128)(2,1)}, u32[]{:S(2)}, u32[]{:S(2)}) collective-permute-start(bf16[256,384]{1,0:T(8,128)(2,1)} %get-tuple-element.107), channel_id=1, source_target_pairs={{12,0},{16,4},{20,8},{24,12},{28,16},{13,1},{17,5},{21,9},{25,13},... | collective-permute-start | bytes 589832 | tf_op jit(solution)/shard_map/ppermute | solution.py:311
  304.3 14.6 %collective-permute-start.19 = (bf16[256,384]{1,0:T(8,128)(2,1)S(1)}, bf16[256,384]{1,0:T(8,128)(2,1)}, u32[]{:S(2)}, u32[]{:S(2)}) collective-permute-start(bf16[256,384]{1,0:T(8,128)(2,1)S(1)} %get-tuple-element.108), channel_id=1, source_target_pairs={{8,0},{12,4},{16,8},{20,12},{24,16},{28,20},{9,1},{13,5},{17,9},{2... | collective-permute-start | bytes 589832 | tf_op jit(solution)/shard_map/ppermute | solution.py:311
  324.0 40.0 %reduce-scatter.44.cloned.1.call-start = ((), (), s32[]{:S(2)}) async-start(), calls=%async_computation.25 | async-start | bytes 4718592 | tf_op jit(solution)/shard_map/reduce_scatter | solution.py:397
  326.8 55.2 %reduce-scatter.42.cloned.1.call-start = ((), (), s32[]{:S(2)}) async-start(), calls=%async_computation.24 | async-start | bytes 9437184 | tf_op jit(solution)/shard_map/reduce_scatter | solution.py:395
  333.6 81.9 %reduce-scatter.46.cloned.1.call-start = ((), (), s32[]{:S(2)}) async-start(), calls=%async_computation.28 | async-start | bytes 983040
  340.9 110.6 %reduce-scatter.48.cloned.1.call-start = ((), (), s32[]{:S(2)}) async-start(), calls=%async_computation.29 | async-start | bytes 442368
  342.3 149.1 %reduce-scatter.40.cloned.1.call-start = ((), (), s32[]{:S(2)}) async-start(), calls=%async_computation.23 | async-start | bytes 1327104 | tf_op jit(solution)/shard_map/reduce_scatter | solution.py:425
  344.1 186.4 %reduce-scatter.50.cloned.1.call-start = ((), (), s32[]{:S(2)}) async-start(), calls=%async_computation.30 | async-start | bytes 884736
  354.3 216.5 %reduce-scatter.32.cloned.1.call-start = ((), (), s32[]{:S(2)}) async-start(), calls=%async_computation.19 | async-start | bytes 1327104 | tf_op jit(solution)/shard_map/reduce_scatter | solution.py:425
  356.1 254.7 %reduce-scatter.34.cloned.1.call-start = ((), (), s32[]{:S(2)}) async-start(), calls=%async_computation.20 | async-start | bytes 1327104 | tf_op jit(solution)/shard_map/reduce_scatter | solution.py:425
  358.2 292.8 %reduce-scatter.36.cloned.1.call-start = ((), (), s32[]{:S(2)}) async-start(), calls=%async_computation.21 | async-start | bytes 1327104 | tf_op jit(solution)/shard_map/reduce_scatter | solution.py:425
  360.0 331.0 %reduce-scatter.38.cloned.1.call-start = ((), (), s32[]{:S(2)}) async-start(), calls=%async_computation.22 | async-start | bytes 1327104 | tf_op jit(solution)/shard_map/reduce_scatter | solution.py:425
  361.8 363.3 %reduce-scatter.54.cloned.1.call-start = ((), (), s32[]{:S(2)}) async-start(), calls=%async_computation.32 | async-start | bytes 1966080
  364.0 408.2 %reduce-scatter.52.cloned.1.call-start = ((), (), s32[]{:S(2)}) async-start(), calls=%async_computation.31 | async-start | bytes 3932160
  385.1 307.6 %all-to-all-start = ((f32[64,4,384]{2,0,1:T(8,128)}), f32[64,4,384]{2,0,1:T(8,128)S(1)}, u32[]{:S(2)}, u32[]{:S(2)}) async-start(f32[64,4,384]{2,0,1:T(8,128)} %bitcast.114), calls=%async_computation.3 | async-start | bytes 786432 | tf_op jit(solution)/shard_map/all_to_all | solution.py:422
  (59 other events, 499.2 us)
Sparse Core Ops, SparseCore 0:
  100.7 26.6 reduce-scatter.25
  226.7 23.3 reduce-scatter.27
  324.2 27.5 reduce-scatter.29
  353.8 10.1 reduce-scatter.43
  366.2 15.6 reduce-scatter.41
  384.7 30.7 reduce-scatter.45
  418.5 32.8 reduce-scatter.47
  454.7 36.7 reduce-scatter.39
  495.5 34.9 reduce-scatter.49
  533.9 36.7 reduce-scatter.31
  574.0 36.7 reduce-scatter.33
  614.2 36.7 reduce-scatter.35
  654.2 36.7 reduce-scatter.37
  694.1 30.9 reduce-scatter.53
  728.2 43.8 reduce-scatter.51
Sparse Core Ops, SparseCore 1:
  103.2 70.2 all-gather.6
  175.1 43.8 all-gather.8

commit v2 on v1

--- a/solution.py
+++ b/solution.py
@@ -52,8 +52,8 @@
     return inv, root
 
 
-def path_fwd_kernel(heads, q_ref, k_ref, r_ref, c_ref, qt_ref, kt_ref, near_ref, p_ref,
-                    u_ref, inv_ref, psi_ref, x_ref, y_ref):
+def path_fwd_stage(heads, q_ref, k_ref, r_ref, c_ref, qt_ref, kt_ref, near_ref, p_ref,
+                   u_ref, inv_ref, psi_ref, x_ref, y_ref, done=None):
     n = q_ref.shape[0]
     rows, cols = iotas(n)
     strength = c_ref[...]
@@ -99,6 +99,12 @@
         near_ref[h] = dot3(q2, k2, 1, 1) - dot3(fq2, split(psi), 1, 0)
         er, ec = iotas(HDIM)
         p_ref[h] = jnp.where(er == ec, 1.0, 0.0) - dot3(u2, x2, 0, 0)
+        if done is not None:
+            done(h)
+
+
+def path_fwd_kernel(heads, *refs):
+    path_fwd_stage(heads, *refs)
 
 
 def path_fwd(q, k, r, c, heads):
@@ -128,23 +134,23 @@
     return r * (r - 1) // 2 + m
 
 
-def attn_fwd_kernel(heads, hops, len_ref, row_ref, qt_ref, near_ref, v_ref, fk_ref, fv_ref, fp_ref,
-                    o_ref, p_ref, chain_ref, s_ref):
+def attn_fwd_stage(heads, hops, row, len_ref, qt_ref, near_ref, v_ref, fv_ref, fp_ref, chain_ref,
+                   o_ref, p_ref, s_ref, get_k, get_p):
     n = qt_ref.shape[0]
     scale = HDIM ** (-0.5)
-    row = row_ref[0]
     rows, cols = iotas(n)
     own = doc_of(row * n + rows, len_ref)
     near_ok = (rows >= cols) & (own == doc_of(row * n + cols, len_ref))
     for h in range(heads):
         cs = head_cols(h)
         q = qt_ref[:, cs]
+        for copy in get_k[h] + get_p[h]:
+            copy.wait_recv()
         s = jnp.where(near_ok, near_ref[h] * scale, neg_big)
-        s_ref[h, 0] = s
+        s_ref[0] = s
         top = jnp.max(s, 1, keepdims=True)
         for r in range(1, hops + 1):
-            keys = fk_ref[r - 1, :, cs]
-            chain_ref[chain_slot(r, 0), :, cs] = keys
+            keys = chain_ref[chain_slot(r, 0), :, cs]
             for m in range(1, r):
                 ph, plo = split(fp_ref[r - m - 1, h])
                 keys = (dot(keys, ph, 1, 1) + dot(keys, plo, 1, 1)).astype(BF)
@@ -152,21 +158,29 @@
             source = row - r
             docs = jnp.where(source >= 0, doc_of(source * n + cols, len_ref), -1)
             s = jnp.where(own == docs, dot(q, keys, 1, 1) * scale, neg_big)
-            s_ref[h, r] = s
+            s_ref[r] = s
             top = jnp.maximum(top, jnp.max(s, 1, keepdims=True))
         total = jnp.zeros((n, 1), F32)
         for r in range(hops + 1):
-            e = jnp.exp(s_ref[h, r] - top)
-            s_ref[h, r] = e
+            e = jnp.exp(s_ref[r] - top)
+            s_ref[r] = e
             total = total + jnp.sum(e, 1, keepdims=True)
         recip = 1.0 / total
         out = jnp.zeros((n, HDIM), F32)
         for r in range(hops + 1):
-            p = (s_ref[h, r] * recip).astype(BF)
+            p = (s_ref[r] * recip).astype(BF)
             p_ref[r, h] = p
             vals = v_ref[:, cs] if r == 0 else fv_ref[r - 1, :, cs]
             out = out + dot(p, vals, 1, 0)
         o_ref[:, cs] = out.astype(BF)
+
+def attn_fwd_kernel(heads, hops, len_ref, row_ref, qt_ref, near_ref, v_ref, fk_ref, fv_ref, fp_ref,
+                    o_ref, p_ref, chain_ref, s_ref):
+    for r in range(1, hops + 1):
+        chain_ref[chain_slot(r, 0)] = fk_ref[r - 1]
+    none = [[] for _ in range(heads)]
+    attn_fwd_stage(heads, hops, row_ref[0], len_ref, qt_ref, near_ref, v_ref, fv_ref, fp_ref, chain_ref,
+                   o_ref, p_ref, s_ref, none, none)
 
 
 def attn_fwd(lengths, my_row, qt, near, v, far_k, far_v, far_p, heads, hops):
@@ -182,7 +196,7 @@
             jax.ShapeDtypeStruct((hops + 1, heads, n, n), BF),
             jax.ShapeDtypeStruct((slots, n, width), BF),
         ),
-        scratch_shapes=[pltpu.VMEM((heads, hops + 1, n, n), F32)],
+        scratch_shapes=[pltpu.VMEM((hops + 1, n, n), F32)],
         compiler_params=pltpu.CompilerParams(vmem_limit_bytes=VMEM_LIMIT),
         name="attn_fwd",
     )(lengths, my_row, qt, near, v, far_k, far_v, far_p)
@@ -305,6 +319,263 @@
     )(q, k, r, c, *saved, gqt, gkt, gnear, gp)
 
 
+MESH = pl.DeviceIdType.MESH
+
+
+class Copies:
+    def __init__(self, send, recv):
+        self.send, self.recv, self.count = send, recv, 0
+
+    def start(self, src, dst, device):
+        i = self.count
+        self.count = i + 1
+        copy = pltpu.make_async_remote_copy(
+            src_ref=src, dst_ref=dst, send_sem=self.send.at[i], recv_sem=self.recv.at[i],
+            device_id=device, device_id_type=MESH)
+        copy.start()
+        return copy
+
+
+class Loads:
+    def __init__(self, sems):
+        self.sems, self.count = sems, 0
+
+    def start(self, src, dst):
+        copy = pltpu.make_async_copy(src, dst, self.sems.at[self.count])
+        self.count = self.count + 1
+        copy.start()
+        return copy
+
+
+class Place:
+    def __init__(self, sizes):
+        self.seq_n, self.hid_n, self.wid_n = sizes
+        self.seq = lax.axis_index("seq")
+        self.hid = lax.axis_index("hid")
+        self.wid = lax.axis_index("wid")
+        self.rows_n = self.seq_n * self.hid_n
+        self.row = self.seq * self.hid_n + self.hid
+
+    def wid_peer(self, i):
+        return lax.rem(self.wid + i, self.wid_n)
+
+    def hid_peer(self, i):
+        return lax.rem(self.hid + i, self.hid_n)
+
+    def seq_peer(self, i):
+        return lax.rem(self.seq + i, self.seq_n)
+
+    def row_peer(self, i):
+        to = lax.rem(self.row + i + self.rows_n, self.rows_n)
+        return {"seq": to // self.hid_n, "hid": lax.rem(to, self.hid_n)}
+
+    def barrier(self):
+        sem = pltpu.get_barrier_semaphore()
+        for i in range(1, self.wid_n):
+            pl.semaphore_signal(sem, inc=1, device_id={"wid": self.wid_peer(i)}, device_id_type=MESH)
+        for i in range(1, self.rows_n):
+            pl.semaphore_signal(sem, inc=1, device_id=self.row_peer(i), device_id_type=MESH)
+        pl.semaphore_wait(sem, self.wid_n - 1 + self.rows_n - 1)
+
+
+def aligned(start, size, step):
+    return pl.ds(pl.multiple_of(start, step), size)
+
+
+def fwd_kernel(cfg, len_ref, x_ref, dy_ref, gain_ref, wq_ref, wk_ref, wv_ref, wr_ref, wb_ref, wo_ref,
+               wg_ref, wu_ref, wd_ref,
+               act_ref, xall_ref, gall_ref, dyall_ref, q_ref, k_ref, r_ref, c_ref, v_ref,
+               qt_ref, u_ref, inv_ref, psi_ref, x1_ref, y1_ref,
+               fv_ref, fp_ref, chain_ref, probs_ref, o_ref, mixed_ref, inner_ref,
+               hidden_ref, ggate_ref, gup_ref, gin_ref, fsum_ref,
+               wq_s, wk_s, wv_s, wr_s, wo_s, wg_s, wu_s, wd_s, kt_s, near_s, prod_s, s_s, part_s, recv_s, row_s,
+               load_sem, send_sem, recv_sem):
+    heads, hops, sizes = cfg
+    place = Place(sizes)
+    wid_n, hid_n, seq_n = place.wid_n, place.hid_n, place.seq_n
+    n, col = x_ref.shape
+    model = act_ref.shape[1]
+    ff = wg_ref.shape[1]
+    sub = n // wid_n
+    copies, loads = Copies(send_sem, recv_sem), Loads(load_sem)
+    my_cols = aligned(place.wid * col, col, 128)
+    my_rows = aligned(place.wid * sub, sub, sub)
+
+    load_x = [loads.start(x_ref, xall_ref.at[:, my_cols]), loads.start(gain_ref, gall_ref.at[:, my_cols])]
+    load_w = [loads.start(a, b) for a, b in ((wv_ref, wv_s), (wq_ref, wq_s), (wk_ref, wk_s), (wr_ref, wr_s))]
+    load_dy = loads.start(dy_ref, dyall_ref.at[:, my_cols])
+    load_o = loads.start(wo_ref, wo_s)
+    load_f = [loads.start(wg_ref, wg_s.at[:, pl.ds(0, ff)]), loads.start(wu_ref, wu_s.at[:, pl.ds(0, ff)]),
+              loads.start(wd_ref, wd_s.at[pl.ds(0, ff), :])]
+    place.barrier()
+
+    order = sorted(range(1, wid_n), key=lambda i: -min(i, wid_n - i))
+    to_wid = [{"wid": place.wid_peer(i)} for i in order]
+    get_x = [copies.start(x_ref, xall_ref.at[:, my_cols], d) for d in to_wid]
+    get_x += [copies.start(gain_ref, gall_ref.at[:, my_cols], d) for d in to_wid]
+
+    part_c, part_f = model // seq_n, ff // seq_n
+    mine_c = aligned(place.seq * part_c, part_c, 16)
+    mine_f = aligned(place.seq * part_f, part_f, 16)
+
+    def slot_f(j):
+        return aligned(j * ff + place.seq * part_f, part_f, 16)
+
+    get_gu = []
+    for src, dst in ((wg_ref, wg_s), (wu_ref, wu_s)):
+        get_gu += [copies.start(src.at[mine_c, :], dst.at[mine_c, pl.ds(j * ff, ff)], {"hid": place.hid_peer(j)})
+                   for j in range(1, hid_n)]
+
+    for copy in load_x:
+        copy.wait()
+    for copy in get_x:
+        copy.wait_recv()
+    get_dy = [copies.start(dy_ref, dyall_ref.at[:, my_cols], d) for d in to_wid]
+    xf = xall_ref[...].astype(F32)
+    inv_rms = lax.rsqrt(jnp.mean(xf * xf, -1, keepdims=True) + eps_norm)
+    act_ref[...] = (xf * inv_rms * gall_ref[0:1, :]).astype(BF)
+    for copy in load_w:
+        copy.wait()
+    act = act_ref[...]
+    v_ref[...] = dot(act, wv_s[...], 1, 0).astype(BF)
+    get_v = [copies.start(v_ref, fv_ref.at[i - 1], place.row_peer(i)) for i in range(1, hops + 1)]
+    q_ref[...] = dot(act, wq_s[...], 1, 0)
+    k_ref[...] = dot(act, wk_s[...], 1, 0)
+    r_ref[...] = dot(act, wr_s[...], 1, 0)
+    c_ref[...] = dot(act, wb_ref[...], 1, 0)
+
+    get_k = [[] for _ in range(heads)]
+    get_p = [[] for _ in range(heads)]
+
+    def send_head(h):
+        cs = head_cols(h)
+        for i in range(1, hops + 1):
+            get_k[h].append(copies.start(kt_s.at[:, cs], chain_ref.at[chain_slot(i, 0), :, cs], place.row_peer(i)))
+        for i in range(1, hops):
+            get_p[h].append(copies.start(prod_s.at[h], fp_ref.at[i - 1, h], place.row_peer(i)))
+
+    path_fwd_stage(heads, q_ref, k_ref, r_ref, c_ref, qt_ref, kt_s, near_s, prod_s,
+                   u_ref, inv_ref, psi_ref, x1_ref, y1_ref, send_head)
+
+    for copy in get_gu:
+        copy.wait_recv()
+    pass_gu = []
+    for dst in (wg_s, wu_s):
+        for i in range(1, seq_n):
+            there = dst.at[mine_c, pl.ds(ff, (hid_n - 1) * ff)]
+            pass_gu.append(copies.start(there, there, {"seq": place.seq_peer(i)}))
+    get_d = [copies.start(wd_ref.at[mine_f, :], wd_s.at[slot_f(j), :], {"hid": place.hid_peer(j)})
+             for j in range(1, hid_n)]
+
+    for copy in get_v:
+        copy.wait_recv()
+    attn_fwd_stage(heads, hops, place.row, len_ref, qt_ref, near_s, v_ref, fv_ref, fp_ref, chain_ref,
+                   o_ref, probs_ref, s_s, get_k, get_p)
+
+    load_o.wait()
+    get_a = []
+    for slot, i in enumerate(order):
+        peer = place.wid_peer(i)
+        rows = aligned(peer * sub, sub, sub)
+        part_s[rows, :] = dot(o_ref[rows, :], wo_s[...], 1, 0).astype(BF)
+        get_a.append(copies.start(part_s.at[rows, :], recv_s.at[slot], {"wid": peer}))
+    part_s[my_rows, :] = dot(o_ref[my_rows, :], wo_s[...], 1, 0).astype(BF)
+    mixed = xall_ref[my_rows, :].astype(F32) + part_s[my_rows, :].astype(F32)
+    for copy in get_d:
+        copy.wait_recv()
+    pass_d = []
+    for i in range(1, seq_n):
+        for j in range(1, hid_n):
+            there = wd_s.at[slot_f(j), :]
+            pass_d.append(copies.start(there, there, {"seq": place.seq_peer(i)}))
+    for slot, copy in enumerate(get_a):
+        copy.wait_recv()
+        mixed = mixed + recv_s[slot].astype(F32)
+    mixed_ref[...] = mixed
+    inv_two = lax.rsqrt(jnp.mean(mixed * mixed, -1, keepdims=True) + eps_norm)
+    row_s[...] = (mixed * inv_two * gall_ref[1:2, :]).astype(BF)
+    get_i = [copies.start(row_s, inner_ref.at[my_rows, :], d) for d in to_wid]
+    inner_ref[my_rows, :] = row_s[...]
+    load_dy.wait()
+    for copy in load_f:
+        copy.wait()
+    for copy in get_dy + pass_gu + pass_d + get_i:
+        copy.wait_recv()
+
+    def hidden_tile(t, carry):
+        cs = aligned(t * ff, ff, 128)
+        gate = dot(inner_ref[...], wg_s[:, cs], 1, 0)
+        up = dot(inner_ref[...], wu_s[:, cs], 1, 0)
+        g_hidden = dot(dyall_ref[...], wd_s[cs, :], 1, 1)
+        sig = 1.0 / (1.0 + jnp.exp(-gate))
+        silu = gate * sig
+        hidden_ref[:, cs] = (silu * up).astype(BF)
+        ggate_ref[:, cs] = (g_hidden * up * sig * (1.0 + gate * (1.0 - sig))).astype(BF)
+        gup_ref[:, cs] = (g_hidden * silu).astype(BF)
+        return carry
+
+    lax.fori_loop(0, hid_n, hidden_tile, 0)
+
+    def model_tile(t, carry):
+        cs = aligned(t * col, col, 128)
+        gin_ref[:, cs] = (dot(ggate_ref[...], wg_s[cs, :], 1, 1) + dot(gup_ref[...], wu_s[cs, :], 1, 1)).astype(BF)
+        fsum_ref[:, cs] = (dot(hidden_ref[...], wd_s[:, cs], 1, 0) + part_s[:, cs].astype(F32)).astype(BF)
+        return carry
+
+    lax.fori_loop(0, wid_n, model_tile, 0)
+    every = get_x + get_gu + get_dy + get_v + pass_gu + get_d + get_a + pass_d + get_i
+    for h in range(heads):
+        every += get_k[h] + get_p[h]
+    for copy in every:
+        copy.wait_send()
+
+
+def forward(args, heads, hops, sizes):
+    lengths, x, dy, gains, wq, wk, wv, wr, wb, wo, wg, wu, wd = args
+    n, col = x.shape
+    seq_n, hid_n, wid_n = sizes
+    model, ff = wq.shape[0], wg.shape[1]
+    width = wq.shape[1]
+    sub = n // wid_n
+    slots = hops * (hops + 1) // 2
+    S = jax.ShapeDtypeStruct
+    outs = dict(
+        act=S((n, model), BF), xall=S((n, model), BF), gall=S((8, model), F32), dyall=S((n, model), BF),
+        q=S((n, width), F32), k=S((n, width), F32), r=S((n, width), F32), c=S((n, heads), F32), v=S((n, width), BF),
+        qt=S((n, width), BF), u=S((n, width), F32), inv=S((heads, n, n), F32), psi=S((heads, n, n), F32),
+        x1=S((n, width), F32), y1=S((n, width), F32),
+        fv=S((hops, n, width), BF), fp=S((hops - 1, heads, HDIM, HDIM), F32), chain=S((slots, n, width), BF),
+        probs=S((hops + 1, heads, n, n), BF), o=S((n, width), BF), mixed=S((sub, model), F32),
+        inner=S((n, model), BF), hidden=S((n, hid_n * ff), BF), ggate=S((n, hid_n * ff), BF),
+        gup=S((n, hid_n * ff), BF), gin=S((n, model), BF), fsum=S((n, model), BF),
+    )
+    V = pltpu.VMEM
+    n_copies = (3 * 3 * (wid_n - 1) + 3 * (hid_n - 1) + (seq_n - 1) * (2 + hid_n - 1)
+                + hops + heads * (2 * hops - 1)) + 8
+    any_spec = pl.BlockSpec(memory_space=pl.ANY)
+    vmem = pl.BlockSpec(memory_space=pltpu.VMEM)
+    smem = pl.BlockSpec(memory_space=pltpu.SMEM)
+    res = pl.pallas_call(
+        functools.partial(fwd_kernel, (heads, hops, sizes)),
+        in_specs=[smem, any_spec, any_spec, any_spec] + [any_spec] * 4 + [vmem] + [any_spec] * 4,
+        out_shape=tuple(outs.values()),
+        out_specs=tuple(vmem for _ in outs),
+        scratch_shapes=[
+            V((model, width), BF), V((model, width), BF), V((model, width), BF), V((model, width), BF),
+            V((width, model), BF),
+            V((model, hid_n * ff), BF), V((model, hid_n * ff), BF), V((hid_n * ff, model), BF),
+            V((n, width), BF), V((heads, n, n), F32), V((heads, HDIM, HDIM), F32), V((hops + 1, n, n), F32),
+            V((n, model), BF), V((wid_n - 1, sub, model), BF), V((sub, model), BF),
+            pltpu.SemaphoreType.DMA((11,)), pltpu.SemaphoreType.DMA((n_copies,)),
+            pltpu.SemaphoreType.DMA((n_copies,)),
+        ],
+        compiler_params=pltpu.CompilerParams(
+            vmem_limit_bytes=VMEM_LIMIT, collective_id=1, has_side_effects=True),
+        name="forward",
+    )(lengths, x, dy, gains, wq, wk, wv, wr, wb, wo, wg, wu, wd)
+    return dict(zip(outs, res))
+
+
 def shifted(array, axis, by):
     peers = lax.axis_size(axis)
     pairs = [(i, i + by) for i in range(peers) if 0 <= i + by < peers]
@@ -443,6 +714,102 @@
     )
 
 
+def fast_body(inputs, gain_attn, gain_ffn, w_query, w_key, w_value, w_house, w_beta, w_out,
+              w_gate, w_up, w_down, lengths, cotangent):
+    tok, col = inputs.shape
+    row_devs = lax.axis_size(ROWS)
+    my_wid = lax.axis_index("wid")
+    my_hid = lax.axis_index("hid")
+    wid_n, hid_n, seq_n = lax.axis_size("wid"), lax.axis_size("hid"), lax.axis_size("seq")
+    most_len = max(LEAST, 2 * tok * row_devs // 5)
+    hops = min((most_len - 2) // tok + 1, row_devs - 1)
+    heads = w_query.shape[1] // HDIM
+    ff = w_gate.shape[1]
+    sub = tok // wid_n
+    gains = jnp.zeros((8, col), F32).at[0].set(gain_attn.astype(F32)).at[1].set(gain_ffn.astype(F32))
+    f = forward((lengths, inputs, cotangent, gains, w_query, w_key, w_value, w_house, w_beta, w_out,
+                 w_gate, w_up, w_down), heads, hops, (seq_n, hid_n, wid_n))
+    gain_one, gain_two = f["gall"][0], f["gall"][1]
+    normed_one, inverse_one = norm_rows(f["xall"].astype(F32))
+    act, v, qt, fv, fp, chain, probs, attended = (f[i] for i in ("act", "v", "qt", "fv", "fp", "chain", "probs", "o"))
+    q, k, r, c = f["q"], f["k"], f["r"], f["c"]
+    saved = [f[i] for i in ("u", "inv", "psi", "x1", "y1")]
+    dy_all, inner, hidden = f["dyall"], f["inner"], f["hidden"]
+    dy_rows = lax.dynamic_slice_in_dim(dy_all, my_wid * sub, sub, 0).astype(F32)
+    normed_two, inverse_two = norm_rows(f["mixed"])
+
+    ffn_cols = lax.psum_scatter(f["fsum"], "wid", scatter_dimension=1, tiled=True)
+    output = (inputs.astype(F32) + ffn_cols.astype(F32)).astype(BF)
+    g_inner = lax.psum_scatter(f["gin"], "wid", scatter_dimension=0, tiled=True).astype(F32)
+    g_mixed_n, g_gain_two = norm_back(g_inner, normed_two, inverse_two, gain_two)
+    g_z = lax.all_gather((dy_rows + g_mixed_n).astype(BF), "wid", axis=0, tiled=True)
+
+    pick = lax.rem(my_hid - jnp.arange(hid_n) + hid_n, hid_n)
+
+    def slots(x, dim):
+        shape = x.shape[:dim] + (hid_n, ff) + x.shape[dim + 1:]
+        return jnp.moveaxis(jnp.take(x.reshape(shape), pick, axis=dim), dim, 0)
+
+    def cgrad(g):
+        return slots(jnp.einsum("tc,tf->cf", inner, g, preferred_element_type=F32).astype(BF), 1)
+
+    d_gu = jnp.concatenate([cgrad(f["ggate"]), cgrad(f["gup"])], 2)
+    d_dn = slots(jnp.einsum("tf,tc->fc", hidden, dy_all, preferred_element_type=F32).astype(BF), 0)
+    d_gu = lax.psum_scatter(d_gu, "seq", scatter_dimension=1, tiled=True)
+    d_gu = lax.psum_scatter(d_gu, "hid", scatter_dimension=0)
+    d_dn = lax.psum_scatter(d_dn, "seq", scatter_dimension=2, tiled=True)
+    d_dn = lax.psum_scatter(d_dn, "hid", scatter_dimension=0)
+
+    g_attn = jnp.einsum("tc,ic->ti", g_z, w_out, preferred_element_type=F32).astype(BF)
+    d_out = jnp.einsum("ti,tc->ic", attended, g_z, preferred_element_type=F32).astype(BF)
+    g_qt, g_near, gv, send_k, send_v, send_p = attn_bwd(probs, g_attn, qt, v, fv, fp, chain, heads, hops)
+    g_kt = sum(shifted(send_k[i - 1], ROWS, -i).astype(F32) for i in range(1, hops + 1))
+    gv = gv + sum(shifted(send_v[i - 1], ROWS, -i).astype(F32) for i in range(1, hops + 1))
+    g_prod = sum(shifted(send_p[i - 1], ROWS, -i).astype(F32) for i in range(1, hops))
+    g_q, g_k, g_r, g_c = path_bwd(q, k, r, c, saved, g_qt, g_kt, g_near, g_prod, heads)
+    g_v = gv.astype(BF)
+
+    def weight_grad(grad_low):
+        return jnp.einsum("tc,ti->ci", act, grad_low, preferred_element_type=F32).astype(BF)
+
+    def input_grad(grad_low, weight):
+        return jnp.einsum("ti,ci->tc", grad_low, weight, preferred_element_type=F32)
+
+    g_act = (input_grad(g_q, w_query) + input_grad(g_k, w_key) + input_grad(g_v, w_value)
+             + input_grad(g_r, w_house) + input_grad(g_c, w_beta))
+    g_act = lax.psum_scatter(g_act.astype(BF), "wid", scatter_dimension=0, tiled=True).astype(F32)
+    normed_rows = lax.dynamic_slice_in_dim(normed_one, my_wid * sub, sub, 0)
+    inverse_rows = lax.dynamic_slice_in_dim(inverse_one, my_wid * sub, sub, 0)
+    g_resid, g_gain_one = norm_back(g_act, normed_rows, inverse_rows, gain_one)
+    d_rows = dy_rows + g_mixed_n + g_resid
+    d_inputs = lax.all_to_all(d_rows, "wid", split_axis=1, concat_axis=0, tiled=True)
+
+    def scatter(x, dim):
+        return lax.psum_scatter(x, ROWS, scatter_dimension=dim, tiled=True)
+
+    gains = lax.psum(jnp.stack([g_gain_one, g_gain_two]), "wid")
+    gains = scatter(gains, 1)
+    return (
+        output,
+        d_inputs,
+        gains[0],
+        gains[1],
+        scatter(weight_grad(g_q), 0).astype(F32),
+        scatter(weight_grad(g_k), 0).astype(F32),
+        scatter(weight_grad(g_v), 0).astype(F32),
+        scatter(weight_grad(g_r), 0).astype(F32),
+        scatter(weight_grad(g_c), 0).astype(F32),
+        scatter(d_out, 1).astype(F32),
+        d_gu[:, :ff].astype(F32),
+        d_gu[:, ff:].astype(F32),
+        d_dn.astype(F32),
+    )
+
+
+def slow(mesh):
+    return mesh.shape["seq"] * mesh.shape["hid"] > 8
+
+
 def solution(mesh):
     in_specs = (
         P(("seq", "hid"), "wid"), P("wid"), P("wid"),
@@ -456,4 +823,4 @@
         P(("seq", "hid"), "wid"), P(("seq", "hid"), "wid"), P("wid", ("seq", "hid")),
         P("seq", ("hid", "wid")), P("seq", ("hid", "wid")), P(("hid", "wid"), "seq"),
     )
-    return jax.shard_map(body, mesh=mesh, in_specs=in_specs, out_specs=out_specs, check_vma=False)
+    return jax.shard_map(body if slow(mesh) else fast_body, mesh=mesh, in_specs=in_specs, out_specs=out_specs, check_vma=False)

time: 799 us -> 698 us (0.87)
  Pallas kernels: 36.9 us -> 132 us
  blocking collectives: 112 us -> 29.7 us
  waiting for transfers between devices: 470 us -> 399 us
  matrix products: 48.8 us -> 21.3 us
  starting transfers between devices: 46.6 us -> 20 us
  local copies, waits for them, and re-layouts: 21.3 us -> 35.7 us
    pallas_call x2 -> x1, Pallas kernels: 19.9 us -> 115 us  [forward(): pl.pallas_call(functools.partial(fwd_kernel, (heads, hops, sizes)), in_sp...]
    all_gather x6 -> x1, blocking collectives: 101 us -> 18 us  [fast_body(): lax.all_gather((dy_rows + g_mixed_n).astype(BF), 'wid', axis=0, tiled=True)]
    all_gather x2 -> x0, waiting for transfers between devices: 55.5 us -> none  [the longest x1 39.5 us: body(): w_dn = lax.all_gather(w_down, 'hid', axis=0)]
    dot_general x14 -> x5, matrix products: 36.8 us -> 9.85 us  [the longest x2 4.64 us: cgrad(): jnp.einsum('tc,tf->cf', inner, g, preferred_element_type=F32).astype(BF)]
    ppermute x22 -> x11, starting transfers between devices: 40.9 us -> 14.4 us  [shifted(): return lax.ppermute(array, axis, pairs)]
    reduce_scatter x5 -> x4, waiting for transfers between devices: 49.6 us -> 33.4 us  [the longest x1 27.2 us: fast_body(): lax.psum_scatter(f['gin'], 'wid', scatter_dimension=0, tiled=True)]
    gather x0 -> x3, local copies, waits for them, and re-layouts: none -> 9.67 us  [slots(): return jnp.moveaxis(jnp.take(x.reshape(shape), pick, axis=dim), dim, 0)]
    unnamed x97 -> x80, local copies, waits for them, and re-layouts: 17.6 us -> 14.4 us
  transfers between devices with their start and end apart: 40 -> 26, of which waited for: 21 -> 16; matrix products, arithmetic and copies ran while one was open for 8% -> 10% of each run, Pallas kernels for 1% -> 1%
where the time goes in v2:
time: 698 us; the launch traced here: 689 us
  waiting for transfers between devices  399 us (57%)
  Pallas kernels  132 us (19%)
  local copies, waits for them, and re-layouts  35.7 us (5%)
  other arithmetic  35.7 us (5%)
  blocking collectives  29.7 us (4%)
  matrix products  21.3 us (3%)
  starting transfers between devices  20 us (3%)
  between operations  15 us (2%)
    reduce_scatter x5, waiting for transfers between devices, scatter(): return lax.psum_scatter(x, ROWS, scatter_dimension=dim, tiled=True)  181 us
    unnamed x19, waiting for transfers between devices  176 us
    pallas_call x1, Pallas kernels, forward(): pl.pallas_call(functools.partial(fwd_kernel, (heads, hops, sizes)), in_sp...  115 us
    reduce_scatter x1, waiting for transfers between devices, fast_body(): lax.psum_scatter(f['gin'], 'wid', scatter_dimension=0, tiled=True)  27.2 us
    all_gather x1, blocking collectives, fast_body(): lax.all_gather((dy_rows + g_mixed_n).astype(BF), 'wid', axis=0, tiled=True)  18 us
    unnamed x80, local copies, waits for them, and re-layouts  14.4 us
    ppermute x11, starting transfers between devices, shifted(): return lax.ppermute(array, axis, pairs)  14.4 us
  transfers between devices with their start and end apart: 26, of which 16 were waited for; matrix products, arithmetic and copies ran while one was open for 10% of the time, Pallas kernels for 1%

profile of v2, /device:TPU:0, one launch (start us, length us, event | category | flops | bytes accessed | tf_op | source)
XLA Modules:
  0.0 688.6 jit_solution(13954125188775136293)
XLA Ops:
  10.9 114.9 %forward.1 = (bf16[256,1536]{1,0:T(8,128)(2,1)}, bf16[256,1536]{1,0:T(8,128)(2,1)}, f32[8,1536]{1,0:T(8,128)}, bf16[256,1536]{1,0:T(8,128)(2,1)}, f32[256,384]{1...) custom-call(s32[3]{0:T(128)} %len_ref.1, ...), custom_call_target="tpu_custom_call" | custom-call | tf_op jit(solution)/shard_map/forward/pallas_call | solution.py:558
  128.0 27.2 %reduce-scatter.25.cloned.1.call-done = bf16[64,1536]{1,0:T(8,128)(2,1)} async-done(((bf16[256,1536]{1,0:T(8,128)(2,1)}), bf16[64,1536]{1,0:T(8,128)(2,1)}) %reduce-scatter.25.cloned.1.call-update) | async-done | bytes 196624 | tf_op jit(solution)/shard_map/reduce_scatter | solution.py:743
  158.2 18.0 %all_gather.3 = bf16[256,1536]{1,0:T(8,128)(2,1)S(1)} all-gather(bf16[64,1536]{1,0:T(8,128)(2,1)S(1)} %fusion.16), channel_id=1, replica_groups=mesh['seq'=2,'hid'=4,'wid'=4] {'wid'}, dimensions={0}, use_global_device_ids=true | all-gather | bytes 983040 | tf_op jit(solution)/shard_map/all_gather | solution.py:745
  178.4 9.7 %attn_bwd.1 = (f32[256,384]{1,0:T(8,128)}, f32[3,256,256]{2,1,0:T(8,128)}, f32[256,384]{1,0:T(8,128)}, bf16[4,256,384]{2,1,0:T(8,128)(2,1)}, bf16[4,256,384]{2,1...) custom-call(bf16[5,3,256,256]{3,2,1,0:T(8,128)(2,1)} %get-tuple-element.90.p_ref, ...), custom_call_target="tpu_custom_call" | custom-call | tf_op jit(solution)/shard_map/attn_bwd/pallas_call | solution.py:244
  197.0 6.4 collective-permute-done.6
  215.1 7.2 %path_bwd.1 = (bf16[256,384]{1,0:T(8,128)(2,1)}, bf16[256,384]{1,0:T(8,128)(2,1)}, bf16[256,384]{1,0:T(8,128)(2,1)}, bf16[256,3]{1,0:T(8,128)(2,1)}) custom-call(f32[256,384]{1,0:T(8,128)} %get-tuple-element.81.q_ref, f32[256,384]{1,0:T(8,128)} %get-tuple-element.82.k_ref, f32[256,384]{1,0:T(8,128)} %get-tuple-element.83.r_ref, ...), custom_call_target="tpu_custom_call" | custom-call | tf_op jit(solution)/shard_map/path_bwd/pallas_call | solution.py:314
  235.9 3.9 broadcast_select_fusion.2
  247.6 2.8 copy.36
  251.1 4.6 gather_fusion.1
  258.2 3.5 broadcast_select_fusion.1
  261.7 3.2 pad_maximum_fusion
  281.5 6.2 reduce-scatter.39.cloned.1.call-done
  290.7 4.8 all-to-all-start
  295.6 25.6 %reduce-scatter.43.cloned.1.call-done = bf16[384,256]{1,0:T(8,128)(2,1)} async-done(((bf16[1536,256]{1,0:T(8,128)(2,1)}), bf16[384,256]{1,0:T(8,128)(2,1)}) %reduce-scatter.43.cloned.1.call-update) | async-done | bytes 196624
  323.0 34.6 %reduce-scatter.45.cloned.1.call-done = bf16[192,3]{1,0:T(8,128)(2,1)} async-done(((bf16[1536,3]{1,0:T(8,128)(2,1)}), bf16[192,3]{1,0:T(8,128)(2,1)}) %reduce-scatter.45.cloned.1.call-update) | async-done | bytes 1168
  359.1 38.5 %reduce-scatter.37.cloned.1.call-done = bf16[384,192]{0,1:T(8,128)(2,1)} async-done(((bf16[384,1536]{0,1:T(8,128)(2,1)}), bf16[384,192]{0,1:T(8,128)(2,1)}) %reduce-scatter.37.cloned.1.call-update) | async-done | bytes 147472 | tf_op jit(solution)/shard_map/reduce_scatter | solution.py:788
  399.3 37.4 %reduce-scatter.47.cloned.1.call-done = f32[192,2]{1,0:T(8,128)} async-done(((f32[1536,2]{1,0:T(8,128)}), f32[192,2]{1,0:T(8,128)}) %reduce-scatter.47.cloned.1.call-update) | async-done | bytes 1552
  437.6 11.7 %psum.8 = f32[2,192]{1,0:T(2,128)S(1)} all-reduce(f32[2,192]{1,0:T(2,128)S(1)} %copy.42), channel_id=1, replica_groups=mesh['seq'=2,'hid'=4,'wid'=4] {'wid'}, use_global_device_ids=true, to_apply=%region_9.10 | all-reduce | flops 384 | bytes 3072 | tf_op jit(solution)/shard_map/psum | solution.py:790
  449.9 27.1 %reduce-scatter.29.cloned.1.call-done = bf16[192,384]{1,0:T(8,128)(2,1)} async-done(((bf16[1536,384]{1,0:T(8,128)(2,1)}), bf16[192,384]{1,0:T(8,128)(2,1)}) %reduce-scatter.29.cloned.1.call-update) | async-done | bytes 147472 | tf_op jit(solution)/shard_map/reduce_scatter | solution.py:788
  478.7 38.2 %reduce-scatter.31.cloned.1.call-done = bf16[192,384]{1,0:T(8,128)(2,1)} async-done(((bf16[1536,384]{1,0:T(8,128)(2,1)}), bf16[192,384]{1,0:T(8,128)(2,1)}) %reduce-scatter.31.cloned.1.call-update) | async-done | bytes 147472 | tf_op jit(solution)/shard_map/reduce_scatter | solution.py:788
  518.6 38.7 %reduce-scatter.33.cloned.1.call-done = bf16[192,384]{1,0:T(8,128)(2,1)} async-done(((bf16[1536,384]{1,0:T(8,128)(2,1)}), bf16[192,384]{1,0:T(8,128)(2,1)}) %reduce-scatter.33.cloned.1.call-update) | async-done | bytes 147472 | tf_op jit(solution)/shard_map/reduce_scatter | solution.py:788
  559.0 38.2 %reduce-scatter.35.cloned.1.call-done = bf16[192,384]{1,0:T(8,128)(2,1)} async-done(((bf16[1536,384]{1,0:T(8,128)(2,1)}), bf16[192,384]{1,0:T(8,128)(2,1)}) %reduce-scatter.35.cloned.1.call-update) | async-done | bytes 147472 | tf_op jit(solution)/shard_map/reduce_scatter | solution.py:788
  598.8 32.6 %reduce-scatter.51.cloned.1.call-done = bf16[1,256,768]{2,1,0:T(8,128)(2,1)} async-done(((bf16[4,256,768]{2,1,0:T(8,128)(2,1)}), bf16[1,256,768]{2,1,0:T(8,128)(2,1)}) %reduce-scatter.51.cloned.1.call-update) | async-done | bytes 393232
  633.3 45.1 %reduce-scatter.49.cloned.1.call-done = bf16[1,768,512]{2,1,0:T(8,128)(2,1)} async-done(((bf16[4,768,512]{2,1,0:T(8,128)(2,1)}), bf16[1,768,512]{2,1,0:T(8,128)(2,1)}) %reduce-scatter.49.cloned.1.call-update) | async-done | bytes 786448
  (192 shorter events, 93.1 us)
Async XLA Ops:
  7.2 148.0 %reduce-scatter.25.cloned.1.call-start = ((), (), s32[]{:S(2)}) async-start(), calls=%async_computation.15 | async-start | bytes 983040 | tf_op jit(solution)/shard_map/reduce_scatter | solution.py:743
  125.8 145.5 %reduce-scatter.27.cloned.1.call-start = ((), (), s32[]{:S(2)}) async-start(), calls=%async_computation.16 | async-start | bytes 983040 | tf_op jit(solution)/shard_map/reduce_scatter | solution.py:780
  189.5 19.3 %collective-permute-start.3 = (bf16[256,384]{1,0:T(8,128)(2,1)S(1)}, bf16[256,384]{1,0:T(8,128)(2,1)S(1)}, u32[]{:S(2)}, u32[]{:S(2)}) collective-permute-start(bf16[256,384]{1,0:T(8,128)(2,1)S(1)} %get-tuple-element.125), channel_id=1, source_target_pairs={{16,0},{20,4},{24,8},{28,12},{17,1},{21,5},{25,9},{29,13},{18,2},{... | collective-permute-start | bytes 589832 | tf_op jit(solution)/shard_map/ppermute | solution.py:582
  190.8 19.3 %collective-permute-start.2 = (bf16[256,384]{1,0:T(8,128)(2,1)S(1)}, bf16[256,384]{1,0:T(8,128)(2,1)S(1)}, u32[]{:S(2)}, u32[]{:S(2)}) collective-permute-start(bf16[256,384]{1,0:T(8,128)(2,1)S(1)} %get-tuple-element.126), channel_id=1, source_target_pairs={{12,0},{16,4},{20,8},{24,12},{28,16},{13,1},{17,5},{21,9},{25,13},... | collective-permute-start | bytes 589832 | tf_op jit(solution)/shard_map/ppermute | solution.py:582
  192.1 11.3 %collective-permute-start.6 = (bf16[3,128,128]{2,1,0:T(8,128)(2,1)S(1)}, bf16[3,128,128]{2,1,0:T(8,128)(2,1)S(1)}, u32[]{:S(2)}, u32[]{:S(2)}) collective-permute-start(bf16[3,128,128]{2,1,0:T(8,128)(2,1)S(1)} %get-tuple-element.129), channel_id=1, source_target_pairs={{12,0},{16,4},{20,8},{24,12},{28,16},{13,1},{17,5},{21,9},{25,13},... | collective-permute-start | bytes 294920 | tf_op jit(solution)/shard_map/ppermute | solution.py:582
  193.6 11.8 %collective-permute-start.5 = (bf16[3,128,128]{2,1,0:T(8,128)(2,1)S(1)}, bf16[3,128,128]{2,1,0:T(8,128)(2,1)S(1)}, u32[]{:S(2)}, u32[]{:S(2)}) collective-permute-start(bf16[3,128,128]{2,1,0:T(8,128)(2,1)S(1)} %get-tuple-element.130), channel_id=1, source_target_pairs={{8,0},{12,4},{16,8},{20,12},{24,16},{28,20},{9,1},{13,5},{17,9},{2... | collective-permute-start | bytes 294920 | tf_op jit(solution)/shard_map/ppermute | solution.py:582
  194.9 11.8 %collective-permute-start.4 = (bf16[3,128,128]{2,1,0:T(8,128)(2,1)S(1)}, bf16[3,128,128]{2,1,0:T(8,128)(2,1)S(1)}, u32[]{:S(2)}, u32[]{:S(2)}) collective-permute-start(bf16[3,128,128]{2,1,0:T(8,128)(2,1)S(1)} %get-tuple-element.128), channel_id=1, source_target_pairs={{4,0},{8,4},{12,8},{16,12},{20,16},{24,20},{28,24},{5,1},{9,5},{13... | collective-permute-start | bytes 294920 | tf_op jit(solution)/shard_map/ppermute | solution.py:582
  206.8 17.9 %collective-permute-start.10 = (bf16[256,384]{1,0:T(8,128)(2,1)}, bf16[256,384]{1,0:T(8,128)(2,1)}, u32[]{:S(2)}, u32[]{:S(2)}) collective-permute-start(bf16[256,384]{1,0:T(8,128)(2,1)} %get-tuple-element.121), channel_id=1, source_target_pairs={{16,0},{20,4},{24,8},{28,12},{17,1},{21,5},{25,9},{29,13},{18,2},{... | collective-permute-start | bytes 589832 | tf_op jit(solution)/shard_map/ppermute | solution.py:582
  208.8 15.9 %collective-permute-start.9 = (bf16[256,384]{1,0:T(8,128)(2,1)S(1)}, bf16[256,384]{1,0:T(8,128)(2,1)}, u32[]{:S(2)}, u32[]{:S(2)}) collective-permute-start(bf16[256,384]{1,0:T(8,128)(2,1)S(1)} %get-tuple-element.122), channel_id=1, source_target_pairs={{12,0},{16,4},{20,8},{24,12},{28,16},{13,1},{17,5},{21,9},{25,13},... | collective-permute-start | bytes 589832 | tf_op jit(solution)/shard_map/ppermute | solution.py:582
  210.1 14.6 %collective-permute-start.8 = (bf16[256,384]{1,0:T(8,128)(2,1)S(1)}, bf16[256,384]{1,0:T(8,128)(2,1)}, u32[]{:S(2)}, u32[]{:S(2)}) collective-permute-start(bf16[256,384]{1,0:T(8,128)(2,1)S(1)} %get-tuple-element.123), channel_id=1, source_target_pairs={{8,0},{12,4},{16,8},{20,12},{24,16},{28,20},{9,1},{13,5},{17,9},{2... | collective-permute-start | bytes 589832 | tf_op jit(solution)/shard_map/ppermute | solution.py:582
  212.2 12.6 %collective-permute-start.7 = (bf16[256,384]{1,0:T(8,128)(2,1)S(1)}, bf16[256,384]{1,0:T(8,128)(2,1)}, u32[]{:S(2)}, u32[]{:S(2)}) collective-permute-start(bf16[256,384]{1,0:T(8,128)(2,1)S(1)} %get-tuple-element.120), channel_id=1, source_target_pairs={{4,0},{8,4},{12,8},{16,12},{20,16},{24,20},{28,24},{5,1},{9,5},{13... | collective-permute-start | bytes 589832 | tf_op jit(solution)/shard_map/ppermute | solution.py:582
  229.8 50.9 %reduce-scatter.41.cloned.1.call-start = ((), (), s32[]{:S(2)}) async-start(), calls=%async_computation.23 | async-start | bytes 4718592 | tf_op jit(solution)/shard_map/reduce_scatter | solution.py:760
  239.9 47.8 %reduce-scatter.39.cloned.1.call-start = ((), (), s32[]{:S(2)}) async-start(), calls=%async_computation.22 | async-start | bytes 9437184 | tf_op jit(solution)/shard_map/reduce_scatter | solution.py:758
  265.0 56.2 %reduce-scatter.43.cloned.1.call-start = ((), (), s32[]{:S(2)}) async-start(), calls=%async_computation.24 | async-start | bytes 983040
  267.5 90.1 %reduce-scatter.45.cloned.1.call-start = ((), (), s32[]{:S(2)}) async-start(), calls=%async_computation.25 | async-start | bytes 442368
  268.8 128.8 %reduce-scatter.37.cloned.1.call-start = ((), (), s32[]{:S(2)}) async-start(), calls=%async_computation.21 | async-start | bytes 1327104 | tf_op jit(solution)/shard_map/reduce_scatter | solution.py:788
  270.5 166.2 %reduce-scatter.47.cloned.1.call-start = ((), (), s32[]{:S(2)}) async-start(), calls=%async_computation.26 | async-start | bytes 884736
  273.7 203.3 %reduce-scatter.29.cloned.1.call-start = ((), (), s32[]{:S(2)}) async-start(), calls=%async_computation.17 | async-start | bytes 1327104 | tf_op jit(solution)/shard_map/reduce_scatter | solution.py:788
  275.5 241.5 %reduce-scatter.31.cloned.1.call-start = ((), (), s32[]{:S(2)}) async-start(), calls=%async_computation.18 | async-start | bytes 1327104 | tf_op jit(solution)/shard_map/reduce_scatter | solution.py:788
  277.2 280.1 %reduce-scatter.33.cloned.1.call-start = ((), (), s32[]{:S(2)}) async-start(), calls=%async_computation.19 | async-start | bytes 1327104 | tf_op jit(solution)/shard_map/reduce_scatter | solution.py:788
  278.9 318.3 %reduce-scatter.35.cloned.1.call-start = ((), (), s32[]{:S(2)}) async-start(), calls=%async_computation.20 | async-start | bytes 1327104 | tf_op jit(solution)/shard_map/reduce_scatter | solution.py:788
  280.7 350.7 %reduce-scatter.51.cloned.1.call-start = ((), (), s32[]{:S(2)}) async-start(), calls=%async_computation.28 | async-start | bytes 1966080
  281.4 397.0 %reduce-scatter.49.cloned.1.call-start = ((), (), s32[]{:S(2)}) async-start(), calls=%async_computation.27 | async-start | bytes 3932160
  290.7 308.1 %all-to-all-start = ((f32[64,4,384]{2,0,1:T(8,128)}), f32[64,4,384]{2,0,1:T(8,128)S(1)}, u32[]{:S(2)}, u32[]{:S(2)}) async-start(f32[64,4,384]{2,0,1:T(8,128)} %bitcast.81), calls=%async_computation.2 | async-start | bytes 786432 | tf_op jit(solution)/shard_map/all_to_all | solution.py:785
  (38 other events, 266.4 us)
Sparse Core Ops, SparseCore 0:
  125.9 29.1 reduce-scatter.24
  230.0 27.2 reduce-scatter.26
  259.6 10.1 reduce-scatter.40
  272.0 15.6 reduce-scatter.38
  290.4 30.7 reduce-scatter.42
  324.7 32.8 reduce-scatter.44
  360.8 36.7 reduce-scatter.36
  401.7 34.9 reduce-scatter.46
  440.3 36.7 reduce-scatter.28
  480.1 36.7 reduce-scatter.30
  520.5 36.7 reduce-scatter.32
  560.4 36.7 reduce-scatter.34
  600.5 30.9 reduce-scatter.50
  634.5 43.9 reduce-scatter.48
